TPU v7x, 32 devices: a whole 2x2x4 slice. The times are simulated.
32 devices in a mesh: group: 2 (over x), ctx: 8 (over z, y), exp: 2 (over core).
Axes of the slice: x: 2, y: 2, z: 4, core: 2. Of those that a mesh axis runs over, the one named last changes fastest.
Arguments:
- prompt_query: bfloat16 [2, 2, 2048, 2048], P('group', 'exp', 'ctx'), may hold values from -6 to 6
- prompt_keys: bfloat16 [2, 2, 2048, 256], P('group', 'exp', 'ctx'), may hold values from -6 to 6
- prompt_values: bfloat16 [2, 2, 2048, 256], P('group', 'exp', 'ctx'), may hold values from -24 to 24
- lengths: int32 [2, 2], P(None, 'exp'), may hold values from 1025 to 2048
- decode_query: bfloat16 [2, 2, 128, 2048], P('group', 'exp', None, 'ctx'), may hold values from -6 to 6
- fresh_keys: bfloat16 [2, 2, 128, 256], P('group', 'exp'), may hold values from -6 to 6
- fresh_values: bfloat16 [2, 2, 128, 256], P('group', 'exp'), may hold values from -24 to 24
- x_dec: bfloat16 [2, 2, 128, 2048], P('group', 'exp', 'ctx'), may hold values from -0.59765625 to 0.59765625
- w_out: bfloat16 [2048, 2048], P('ctx'), may hold values from -0.125 to 0.125
- norm_gain: bfloat16 [2048], replicated, may hold values from 0.5 to 1.5
- w_gate_up: bfloat16 [16, 2048, 1536], P(('ctx', 'exp')), may hold values from -0.125 to 0.125
- w_down: bfloat16 [16, 768, 2048], P(('ctx', 'exp')), may hold values from -0.21875 to 0.21875
- expert_ids: int32 [2, 2, 128, 8], P('group', 'exp', 'ctx'), may hold values from 0 to 15, all different within a row; in each aligned block of 16 rows (0 to 15, 16 to 31, ..., all dimensions but the last counted through in order) at most 16 rows name the same one
- gate_weights: float32 [2, 2, 128, 8], P('group', 'exp', 'ctx'), may hold values from 0.1 to 1
Outputs:
- prompt_attention: bfloat16 [2, 2, 2048, 2048], P('group', 'exp', 'ctx')
- out_dec: bfloat16 [2, 2, 128, 2048], P('group', 'exp', 'ctx')
Inputs may be any that keep to these rules, and one draw needn't show every extreme that they name: `expert_ids`: the 8 experts of a row differ; among the rows of one device no expert is named more than 16 times.
All inputs are finite; a program needn't handle non-finite values.
Results may differ from a plain program's by a relative error of at most 0.025.
Values may be sent and summed in bfloat16 or wider, within the bound.
A program may use at most 128 MiB of HBM per device.

v0:
```python
import math

import jax
import jax.numpy as jnp
from jax import lax
from jax.sharding import PartitionSpec as P

HEAD_SIZE = 128
QUERY_HEADS = 16
KEY_VALUE_HEADS = 2


NEGATIVE_LIMIT = -1e30
EPSILON = 1e-06


def from_partner(block, axis, apart):
    count = lax.axis_size(axis)
    route = []
    for low in range(count):
        high = low | 1 << apart
        if high != low and high < count:
            route += [(low, high), (high, low)]
    return lax.ppermute(block, axis, route)


def blockwise(update, carried, key_row_list, value_row_list, positions, usable):
    row_count = key_row_list.shape[0]
    stride = math.gcd(row_count, 512)
    splits = row_count // stride

    def advance(status, members):
        return (update(status, *members), None)

    shaped = (
        key_row_list.reshape(splits, stride, key_row_list.shape[1]),
        value_row_list.reshape(splits, stride, value_row_list.shape[1]),
        positions.reshape(splits, stride),
        usable.reshape(splits, stride),
    )
    carried, unused_out = lax.scan(advance, carried, shaped)
    return carried


def body(
    prompt_query,
    prompt_keys,
    prompt_values,
    lengths,
    decode_query,
    fresh_keys,
    fresh_values,
    x_dec,
    w_out,
    norm_gain,
    w_gate_up,
    w_down,
    expert_ids,
    gate_weights,
):
    group_width = QUERY_HEADS // KEY_VALUE_HEADS
    scaling = HEAD_SIZE ** (-0.5)
    my_group = lax.axis_index("group")
    ctx_index = lax.axis_index("ctx")
    ctx_count = lax.axis_size("ctx")
    length_list = lengths[:, 0]
    length_mine = lax.dynamic_index_in_dim(length_list, my_group, keepdims=False)
    length_other = lax.dynamic_index_in_dim(length_list, 1 - my_group, keepdims=False)
    token_rows = prompt_query.shape[2]
    prompt_len = token_rows * ctx_count
    query_tensor = prompt_query[0, 0].reshape(token_rows, KEY_VALUE_HEADS, group_width, HEAD_SIZE)
    query_pos = ctx_index * token_rows + lax.iota(jnp.int32, token_rows)
    query_limit = jnp.minimum(length_mine, ctx_index * token_rows + token_rows)
    local_heads = decode_query.shape[3] // HEAD_SIZE
    samples = decode_query.shape[2]
    dec_queries = decode_query[0, 0].reshape(samples, local_heads, HEAD_SIZE)
    kv_head = ctx_index * local_heads // group_width

    def prefill_step(status, key_row_list, value_row_list, positions, usable):
        usable = usable & (positions < query_limit)

        def prefill_compute(carried):
            run_max, run_sum, weighted = carried
            key_parts = key_row_list.reshape(-1, KEY_VALUE_HEADS, HEAD_SIZE)
            value_parts = value_row_list.reshape(-1, KEY_VALUE_HEADS, HEAD_SIZE)
            scores = (
                jnp.einsum(
                    "qhgd,khd->hgqk", query_tensor, key_parts, preferred_element_type=jnp.float32
                )
                * scaling
            )
            keep_mask = usable[None, :] & (positions[None, :] <= query_pos[:, None])
            scores = jnp.where(keep_mask[None, None], scores, NEGATIVE_LIMIT)
            new_max = jnp.maximum(run_max, scores.max(-1))
            rescale = jnp.exp(run_max - new_max)
            weights = jnp.where(keep_mask[None, None], jnp.exp(scores - new_max[..., None]), 0.0)
            run_sum = rescale * run_sum + weights.sum(-1)
            weighted = rescale[..., None] * weighted + jnp.einsum(
                "hgqk,khd->hgqd",
                weights.astype(jnp.bfloat16),
                value_parts,
                preferred_element_type=jnp.float32,
            )
            return (new_max, run_sum, weighted)

        return lax.cond(jnp.any(usable), prefill_compute, lambda carried: carried, status)

    def make_decode():

        def decode_step(status, key_row_list, value_row_list, positions, usable):
            usable = usable & (positions < length_other)

            def decode_compute(carried):
                run_max, run_sum, weighted = carried
                scores = (
                    jnp.einsum(
                        "shd,kd->hsk", dec_queries, key_row_list, preferred_element_type=jnp.float32
                    )
                    * scaling
                )
                scores = jnp.where(usable[None, None], scores, NEGATIVE_LIMIT)
                new_max = jnp.maximum(run_max, scores.max(-1))
                rescale = jnp.exp(run_max - new_max)
                weights = jnp.where(usable[None, None], jnp.exp(scores - new_max[..., None]), 0.0)
                run_sum = rescale * run_sum + weights.sum(-1)
                weighted = rescale[..., None] * weighted + jnp.einsum(
                    "hsk,kd->hsd",
                    weights.astype(jnp.bfloat16),
                    value_row_list,
                    preferred_element_type=jnp.float32,
                )
                return (new_max, run_sum, weighted)

            return lax.cond(jnp.any(usable), decode_compute, lambda carried: carried, status)

        return decode_step

    decode_step = make_decode()
    pre_init = (
        jnp.full((KEY_VALUE_HEADS, group_width, token_rows), NEGATIVE_LIMIT, jnp.float32),
        jnp.zeros((KEY_VALUE_HEADS, group_width, token_rows), jnp.float32),
        jnp.zeros((KEY_VALUE_HEADS, group_width, token_rows, HEAD_SIZE), jnp.float32),
    )
    dec_init = (
        jnp.full((local_heads, samples), NEGATIVE_LIMIT, jnp.float32),
        jnp.zeros((local_heads, samples), jnp.float32),
        jnp.zeros((local_heads, samples, HEAD_SIZE), jnp.float32),
    )
    far_keys, far_values = from_partner((prompt_keys, prompt_values), "group", 0)
    peer_heads = lax.iota(jnp.int32, ctx_count) * local_heads // group_width
    key_chosen = jnp.take(
        far_keys[0, 0].reshape(token_rows, KEY_VALUE_HEADS, HEAD_SIZE), peer_heads, axis=1
    )
    value_chosen = jnp.take(
        far_values[0, 0].reshape(token_rows, KEY_VALUE_HEADS, HEAD_SIZE), peer_heads, axis=1
    )
    head_keys, head_values = (
        lax.all_to_all(key_chosen, "ctx", split_axis=1, concat_axis=0, tiled=True),
        lax.all_to_all(value_chosen, "ctx", split_axis=1, concat_axis=0, tiled=True),
    )
    key_piece = lax.all_gather(prompt_keys, "ctx", axis=2, tiled=True)
    value_piece = lax.all_gather(prompt_values, "ctx", axis=2, tiled=True)
    row_count = key_piece.shape[2]
    positions = lax.iota(jnp.int32, row_count)
    pre_state = blockwise(
        prefill_step, pre_init, key_piece[0, 0], value_piece[0, 0], positions, positions >= 0
    )
    all_positions = lax.iota(jnp.int32, prompt_len)
    dec_state = blockwise(
        make_decode(),
        dec_init,
        head_keys.reshape(prompt_len, HEAD_SIZE),
        head_values.reshape(prompt_len, HEAD_SIZE),
        all_positions,
        all_positions >= 0,
    )
    pre_max, pre_sum, pre_weighted = pre_state
    prompt_attn = pre_weighted / jnp.where(pre_sum > 0, pre_sum, 1.0)[..., None]
    prompt_attn = jnp.transpose(prompt_attn, (2, 0, 1, 3)).reshape(
        token_rows, QUERY_HEADS * HEAD_SIZE
    )
    prompt_attn = jnp.where((query_pos < length_mine)[:, None], prompt_attn, 0.0).astype(
        jnp.bfloat16
    )
    prompt_attention = prompt_attn.reshape(1, 1, token_rows, QUERY_HEADS * HEAD_SIZE)
    dec_max, dec_sum, dec_weighted = dec_state
    own_keys = lax.dynamic_slice_in_dim(fresh_keys[0, 0], kv_head * HEAD_SIZE, HEAD_SIZE, 1)
    own_values = lax.dynamic_slice_in_dim(fresh_values[0, 0], kv_head * HEAD_SIZE, HEAD_SIZE, 1)
    own_score = (
        jnp.einsum("shd,sd->hs", dec_queries, own_keys, preferred_element_type=jnp.float32)
        * scaling
    )
    final_max = jnp.maximum(dec_max, own_score)
    rescale = jnp.exp(dec_max - final_max)
    own_weight = jnp.exp(own_score - final_max)
    dec_sum = rescale * dec_sum + own_weight
    dec_weighted = (
        rescale[..., None] * dec_weighted
        + own_weight.astype(jnp.bfloat16).astype(jnp.float32)[..., None]
        * own_values.astype(jnp.float32)[None]
    )
    dec_attn = (dec_weighted / dec_sum[..., None]).astype(jnp.bfloat16)
    dec_attn = jnp.transpose(dec_attn, (1, 0, 2)).reshape(samples, local_heads * HEAD_SIZE)
    row_count = x_dec.shape[2]
    projected = lax.psum_scatter(
        jnp.dot(dec_attn, w_out, preferred_element_type=jnp.float32).astype(jnp.bfloat16),
        "ctx",
        scatter_dimension=0,
        tiled=True,
    ).astype(jnp.float32)
    residual = x_dec[0, 0].astype(jnp.float32) + projected
    normed = (
        residual
        * lax.rsqrt(jnp.mean(residual * residual, -1, keepdims=True) + EPSILON)
        * norm_gain.astype(jnp.float32)
    ).astype(jnp.bfloat16)
    model_width = normed.shape[1]
    top_count = expert_ids.shape[3]
    n_ctx = lax.axis_size("ctx")
    n_exp = lax.axis_size("exp")
    experts_all = w_gate_up.shape[0] * n_ctx * n_exp
    capacity = max(2, 2 * row_count * top_count // experts_all)
    flat_ids = expert_ids[0, 0].reshape(-1)
    one_hot = (flat_ids[:, None] == lax.iota(jnp.int32, experts_all)[None, :]).astype(jnp.int32)
    earlier = jnp.cumsum(one_hot, 0) - one_hot
    slot_rank = jnp.sum(earlier * one_hot, 1)
    target = flat_ids * capacity + slot_rank
    placing = (
        lax.iota(jnp.int32, experts_all * capacity)[:, None, None]
        == target.reshape(row_count, top_count)[None]
    ).any(-1)
    buffer = jnp.dot(
        placing.astype(jnp.bfloat16), normed, preferred_element_type=jnp.float32
    ).astype(jnp.bfloat16)
    buffer = buffer.reshape(experts_all, capacity, model_width)
    arrived = lax.all_to_all(buffer, ("ctx", "exp"), split_axis=0, concat_axis=0, tiled=True)
    flat_rows = arrived.reshape(-1, model_width)
    mixed = jnp.dot(flat_rows, w_gate_up[0], preferred_element_type=jnp.float32)
    hidden_units = mixed.shape[1] // 2
    hidden = (jax.nn.silu(mixed[:, :hidden_units]) * mixed[:, hidden_units:]).astype(jnp.bfloat16)
    produced = jnp.dot(hidden, w_down[0], preferred_element_type=jnp.float32).astype(jnp.bfloat16)
    outputs = produced.reshape(arrived.shape)
    returned = lax.all_to_all(outputs, ("ctx", "exp"), split_axis=0, concat_axis=0, tiled=True)
    picked = returned.reshape(experts_all * capacity, model_width)[target]
    gate_values = gate_weights[0, 0]
    moe = jnp.sum(
        picked.reshape(row_count, top_count, model_width).astype(jnp.float32)
        * gate_values[..., None],
        1,
    )
    out_dec = (residual + moe).astype(jnp.bfloat16).reshape(1, 1, row_count, model_width)
    return (prompt_attention, out_dec)


def solution(mesh):
    in_specs = (
        P("group", "exp", "ctx", None),
        P("group", "exp", "ctx", None),
        P("group", "exp", "ctx", None),
        P(None, "exp"),
        P("group", "exp", None, "ctx"),
        P("group", "exp", None, None),
        P("group", "exp", None, None),
        P("group", "exp", "ctx", None),
        P("ctx", None),
        P(),
        P(("ctx", "exp"), None, None),
        P(("ctx", "exp"), None, None),
        P("group", "exp", "ctx", None),
        P("group", "exp", "ctx", None),
    )
    out_specs = (P("group", "exp", "ctx", None), P("group", "exp", "ctx", None))
    return jax.shard_map(body, mesh=mesh, in_specs=in_specs, out_specs=out_specs, check_vma=False)
```

profile of v0, /device:TPU:25, one launch (start us, length us, event | category | flops | bytes accessed | tf_op | source)
XLA Modules:
  0.0 324.3 jit_solution(11437767902272269892)
XLA Ops:
  7.2 1.8 copy.74
  9.0 1.2 collective-permute-start.1
  10.2 1.7 copy.71
  12.2 1.4 collective-permute-done.1
  17.6 1.4 gather_fusion.2
  19.0 1.4 gather_fusion.1
  20.4 2.2 select_bitcast_fusion
  22.6 16.7 %all_to_all.40 = bf16[256,8,128]{2,0,1:T(8,128)(2,1)} all-to-all(bf16[256,8,128]{2,0,1:T(8,128)(2,1)S(1)} %get-tuple-element.486), channel_id=1, replica_groups=mesh['group'=2,'ctx'=8,'exp'=2] {'ctx'}, dimensions={1} | all-to-all | bytes 1048576 | tf_op jit(solution)/shard_map/all_to_all | solution.py:158
  39.3 6.3 %all-to-all-start.1 = ((bf16[256,8,128]{2,0,1:T(8,128)(2,1)}), bf16[256,8,128]{2,0,1:T(8,128)(2,1)}, u32[]{:S(2)}, u32[]{:S(2)}) async-start(bf16[256,8,128]{2,0,1:T(8,128)(2,1)} %get-tuple-element.485), calls=%async_computation.1 | async-start | bytes 1048576 | tf_op jit(solution)/shard_map/all_to_all | solution.py:159
  48.9 8.3 %all-to-all-done.1 = bf16[256,8,128]{2,0,1:T(8,128)(2,1)} async-done(((bf16[256,8,128]{2,0,1:T(8,128)(2,1)}), bf16[256,8,128]{2,0,1:T(8,128)(2,1)}, u32[]{:S(2)}, u32[]{:S(2)}) %all-to-all-start.1) | async-done | bytes 524320 | tf_op jit(solution)/shard_map/all_to_all | solution.py:159
  57.3 16.7 %while.31 = (s32[]{:T(128)}, f32[2,128]{1,0:T(2,128)S(1)}, f32[2,128]{1,0:T(2,128)S(1)}, f32[2,128,128]{2,1,0:T(8,128)S(1)}, s32[4,512]{1,0:T(4,128)S(1)}, /*ind...) while((s32[]{:T(128)}, f32[2,128]{1,0:T(2,128)S(1)}, ...), condition=%wide.region_13.15_spmd, body=%wide.region_7.14_spmd.sunk | while | flops 68355584 | bytes 2185460 | solution.py:41
  57.3 1.4 fusion.63
  59.4 2.7 conditional.5
  59.4 1.2 fusion.52
  60.8 1.3 convolution_add_fusion
  62.2 1.4 fusion.63
  64.2 2.7 conditional.5
  64.3 1.2 fusion.52
  65.6 1.3 convolution_add_fusion
  67.0 1.4 fusion.63
  69.1 2.7 conditional.5
  70.5 1.3 convolution_add_fusion
  71.8 1.4 fusion.63
  76.2 2.4 convolution_convert_fusion.1
  81.0 61.8 %reduce-scatter.2.cloned.1.call-done = bf16[16,2048]{1,0:T(8,128)(2,1)} async-done(((bf16[128,2048]{1,0:T(8,128)(2,1)}), bf16[16,2048]{1,0:T(8,128)(2,1)}) %reduce-scatter.2.cloned.1.call-update) | async-done | bytes 65552 | tf_op jit(solution)/shard_map/reduce_scatter | solution.py:205
  143.8 2.4 convolution_convert_fusion
  146.1 7.9 %all-to-all-start.2 = ((bf16[16,16,2048]{2,1,0:T(8,128)(2,1)}), bf16[16,16,2048]{2,1,0:T(8,128)(2,1)}, u32[]{:S(2)}, u32[]{:S(2)}) async-start(bf16[16,16,2048]{2,1,0:T(8,128)(2,1)} %bitcast.131), calls=%async_computation.3 | async-start | bytes 2097152 | tf_op jit(solution)/shard_map/all_to_all | solution.py:236
  154.8 2.3 copy.66
  157.0 2.3 copy.68
  160.8 33.7 %all-gather.3.cloned.1.call-done = bf16[1,1,2048,256]{3,2,1,0:T(8,128)(2,1)} async-done(((bf16[1,1,256,256]{3,2,1,0:T(8,128)(2,1)}), bf16[1,1,2048,256]{3,2,1,0:T(8,128)(2,1)}) %all-gather.3.cloned.1.call-update) | async-done | bytes 1048592 | tf_op jit(solution)/shard_map/all_gather | solution.py:161
  194.4 2.3 copy.67
  196.7 38.9 %all-gather.5.cloned.1.call-done = bf16[1,1,2048,256]{3,2,1,0:T(8,128)(2,1)} async-done(((bf16[1,1,256,256]{3,2,1,0:T(8,128)(2,1)}), bf16[1,1,2048,256]{3,2,1,0:T(8,128)(2,1)}) %all-gather.5.cloned.1.call-update) | async-done | bytes 1048592 | tf_op jit(solution)/shard_map/all_gather | solution.py:162
  235.6 2.3 copy.69
  237.8 4.9 %fusion.28 = f32[256,1536]{1,0:T(8,128)S(1)} fusion(bf16[256,2048]{1,0:T(8,128)(2,1)} %bitcast.38, bf16[1,2048,1536]{2,1,0:T(8,128)(2,1)} %param.34), kind=kOutput, calls=%fused_computation.43 | convolution fusion | flops 1610612736 | bytes 8912896 | tf_op jit(solution)/shard_map/dot_general | solution.py:238
  242.8 2.0 fusion.32
  244.8 8.3 %all-to-all-start.3 = ((bf16[16,16,2048]{2,1,0:T(8,128)(2,1)}), bf16[16,16,2048]{2,1,0:T(8,128)(2,1)}, u32[]{:S(2)}, u32[]{:S(2)}) async-start(bf16[16,16,2048]{2,1,0:T(8,128)(2,1)} %bitcast.134), calls=%async_computation.4 | async-start | bytes 2097152 | tf_op jit(solution)/shard_map/all_to_all | solution.py:243
  253.1 1.6 broadcast_in_dim.115
  254.6 49.1 %while.32 = (s32[]{:T(128)}, f32[2,8,256]{2,1,0:T(8,128)S(1)}, f32[2,8,256]{2,1,0:T(8,128)S(1)}, f32[2,8,256,128]{3,2,1,0:T(8,128)}, s32[4,512]{1,0:T(4,128)S(1)...) while((s32[]{:T(128)}, f32[2,8,256]{2,1,0:T(8,128)S(1)}, ...), condition=%wide.region_6.7_spmd.clone, body=%wide.region_0.0_spmd.clone.sunk | while | flops 1102324992 | bytes 49558864 | solution.py:41
  256.0 11.0 %conditional.6 = ((f32[2,8,256]{2,1,0:T(8,128)S(1)}, f32[2,8,256]{2,1,0:T(8,128)S(1)}, f32[2,8,256,128]{3,2,1,0:T(8,128)})) conditional(s32[]{:T(128)} %convert_element_type.148, (f32[2,8,256]{2,1,0:T(8,128)S(1)}, f32[2,8,256]{2,1,0:T(8,128)S(1)}, f32[2,8,256,128]{3,2,1,0:T(8,128)}) %tuple.99, (pred[512]{0:T(512)(128)(4,1)S(1)}, s32[512]{0:T(512)S(1)}, ...), branch_computations={%region_2.2_spmd, %region_3.5_spmd} | conditional | flops 1102323968 | bytes 49550944 | solution.py:106
  257.3 2.7 fusion.2
  260.0 2.0 fusion.4
  262.1 3.5 %multiply_add_fusion = f32[2,8,256,128]{3,2,1,0:T(8,128)S(1)} fusion(f32[2,8,256,128]{3,2,1,0:T(8,128)S(1)} %copy-done.1, bf16[512,2,128,1]{0,2,3,1:T(8,128)(2,1)S(1)} %bitcast.130, f32[2,512,256,8]{2,1,3,0:T(8,128)S(1)} %get-tuple-element.479, f32[2,8,256]{2,1,0:T(8,128)S(1)} %max.10, pred[256,512]{0,1:T(8,128)(4,1)S(1)} %compare_and_fusion, ...), kind=kOutput, calls=%fused_computation.11 | convolution fusion | flops 548405248 | bytes 13008896 | tf_op jit(solution)/shard_map/while/body/eval_jaxpr/cond/branch_1_fun/hgqk,khd->hgqd/dot_general | solution.py:98
  265.6 1.3 copy-done.2
  268.2 11.0 %conditional.6 = ((f32[2,8,256]{2,1,0:T(8,128)S(1)}, f32[2,8,256]{2,1,0:T(8,128)S(1)}, f32[2,8,256,128]{3,2,1,0:T(8,128)})) conditional(s32[]{:T(128)} %convert_element_type.148, (f32[2,8,256]{2,1,0:T(8,128)S(1)}, f32[2,8,256]{2,1,0:T(8,128)S(1)}, f32[2,8,256,128]{3,2,1,0:T(8,128)}) %tuple.99, (pred[512]{0:T(512)(128)(4,1)S(1)}, s32[512]{0:T(512)S(1)}, ...), branch_computations={%region_2.2_spmd, %region_3.5_spmd} | conditional | flops 1102323968 | bytes 49550944 | solution.py:106
  269.5 2.7 fusion.2
  272.3 2.0 fusion.4
  274.4 3.5 %multiply_add_fusion = f32[2,8,256,128]{3,2,1,0:T(8,128)S(1)} fusion(f32[2,8,256,128]{3,2,1,0:T(8,128)S(1)} %copy-done.1, bf16[512,2,128,1]{0,2,3,1:T(8,128)(2,1)S(1)} %bitcast.130, f32[2,512,256,8]{2,1,3,0:T(8,128)S(1)} %get-tuple-element.479, f32[2,8,256]{2,1,0:T(8,128)S(1)} %max.10, pred[256,512]{0,1:T(8,128)(4,1)S(1)} %compare_and_fusion, ...), kind=kOutput, calls=%fused_computation.11 | convolution fusion | flops 548405248 | bytes 13008896 | tf_op jit(solution)/shard_map/while/body/eval_jaxpr/cond/branch_1_fun/hgqk,khd->hgqd/dot_general | solution.py:98
  277.8 1.3 copy-done.2
  280.5 11.0 %conditional.6 = ((f32[2,8,256]{2,1,0:T(8,128)S(1)}, f32[2,8,256]{2,1,0:T(8,128)S(1)}, f32[2,8,256,128]{3,2,1,0:T(8,128)})) conditional(s32[]{:T(128)} %convert_element_type.148, (f32[2,8,256]{2,1,0:T(8,128)S(1)}, f32[2,8,256]{2,1,0:T(8,128)S(1)}, f32[2,8,256,128]{3,2,1,0:T(8,128)}) %tuple.99, (pred[512]{0:T(512)(128)(4,1)S(1)}, s32[512]{0:T(512)S(1)}, ...), branch_computations={%region_2.2_spmd, %region_3.5_spmd} | conditional | flops 1102323968 | bytes 49550944 | solution.py:106
  281.8 2.7 fusion.2
  284.6 2.0 fusion.4
  286.6 3.5 %multiply_add_fusion = f32[2,8,256,128]{3,2,1,0:T(8,128)S(1)} fusion(f32[2,8,256,128]{3,2,1,0:T(8,128)S(1)} %copy-done.1, bf16[512,2,128,1]{0,2,3,1:T(8,128)(2,1)S(1)} %bitcast.130, f32[2,512,256,8]{2,1,3,0:T(8,128)S(1)} %get-tuple-element.479, f32[2,8,256]{2,1,0:T(8,128)S(1)} %max.10, pred[256,512]{0,1:T(8,128)(4,1)S(1)} %compare_and_fusion, ...), kind=kOutput, calls=%fused_computation.11 | convolution fusion | flops 548405248 | bytes 13008896 | tf_op jit(solution)/shard_map/while/body/eval_jaxpr/cond/branch_1_fun/hgqk,khd->hgqd/dot_general | solution.py:98
  290.1 1.3 copy-done.2
  292.8 11.0 %conditional.6 = ((f32[2,8,256]{2,1,0:T(8,128)S(1)}, f32[2,8,256]{2,1,0:T(8,128)S(1)}, f32[2,8,256,128]{3,2,1,0:T(8,128)})) conditional(s32[]{:T(128)} %convert_element_type.148, (f32[2,8,256]{2,1,0:T(8,128)S(1)}, f32[2,8,256]{2,1,0:T(8,128)S(1)}, f32[2,8,256,128]{3,2,1,0:T(8,128)}) %tuple.99, (pred[512]{0:T(512)(128)(4,1)S(1)}, s32[512]{0:T(512)S(1)}, ...), branch_computations={%region_2.2_spmd, %region_3.5_spmd} | conditional | flops 1102323968 | bytes 49550944 | solution.py:106
  294.1 2.7 fusion.2
  296.9 2.0 fusion.4
  298.9 3.5 %multiply_add_fusion = f32[2,8,256,128]{3,2,1,0:T(8,128)S(1)} fusion(f32[2,8,256,128]{3,2,1,0:T(8,128)S(1)} %copy-done.1, bf16[512,2,128,1]{0,2,3,1:T(8,128)(2,1)S(1)} %bitcast.130, f32[2,512,256,8]{2,1,3,0:T(8,128)S(1)} %get-tuple-element.479, f32[2,8,256]{2,1,0:T(8,128)S(1)} %max.10, pred[256,512]{0,1:T(8,128)(4,1)S(1)} %compare_and_fusion, ...), kind=kOutput, calls=%fused_computation.11 | convolution fusion | flops 548405248 | bytes 13008896 | tf_op jit(solution)/shard_map/while/body/eval_jaxpr/cond/branch_1_fun/hgqk,khd->hgqd/dot_general | solution.py:98
  302.4 1.3 copy-done.2
  303.7 1.9 divide_bitcast_fusion
  305.7 1.6 copy.70
  307.3 2.3 reshape.224
  309.6 2.4 select_convert_fusion
  312.1 3.6 %gather_fusion = bf16[128,2048]{1,0:T(8,128)(2,1)} fusion(bf16[256,2048]{1,0:T(8,128)(2,1)} %bitcast.42, s32[1024]{0:T(1024)S(1)} %pad_clamp_fusion), kind=kCustom, calls=%fused_computation.2 | custom fusion | bytes 1049088 | tf_op jit(solution)/shard_map/gather | solution.py:244
  315.7 1.5 fusion.35
  (141 shorter events, 25.1 us)
Async XLA Ops:
  7.2 235.6 %copy-start = (bf16[1,768,2048]{2,1,0:T(8,128)(2,1)S(1)}, bf16[1,768,2048]{2,1,0:T(8,128)(2,1)}, u32[]{:S(2)}) copy-start(bf16[1,768,2048]{2,1,0:T(8,128)(2,1)} %param.35) | copy-start | bytes 9437188
  7.2 38.4 %copy-start.5 = (bf16[1,1,128,256]{3,2,1,0:T(8,128)(2,1)S(1)}, bf16[1,1,128,256]{3,2,1,0:T(8,128)(2,1)}, u32[]{:S(2)}) copy-start(bf16[1,1,128,256]{3,2,1,0:T(8,128)(2,1)} %param.28) | copy-start | bytes 196612
  7.2 38.8 %copy-start.10 = (bf16[1,1,128,256]{3,2,1,0:T(8,128)(2,1)S(1)}, bf16[1,1,128,256]{3,2,1,0:T(8,128)(2,1)}, u32[]{:S(2)}) copy-start(bf16[1,1,128,256]{3,2,1,0:T(8,128)(2,1)} %param.30) | copy-start | bytes 196612
  7.2 40.4 %copy-start.12 = (s32[2,1]{0,1:T(1,128)S(1)}, s32[2,1]{0,1:T(1,128)}, u32[]{:S(2)}) copy-start(s32[2,1]{0,1:T(1,128)} %param.27) | copy-start | bytes 28
  9.0 4.6 %collective-permute-start.1 = (bf16[1,1,256,256]{2,3,1,0:T(8,128)(2,1)}, bf16[1,1,256,256]{2,3,1,0:T(8,128)(2,1)S(1)}, u32[]{:S(2)}, u32[]{:S(2)}) collective-permute-start(bf16[1,1,256,256]{2,3,1,0:T(8,128)(2,1)} %copy.74), channel_id=1, source_target_pairs={{0,16},{16,0},{1,17},{17,1},{2,18},{18,2},{3,19},{19,3},{4,20},{20... | collective-permute-start | bytes 393224 | tf_op jit(solution)/shard_map/ppermute | solution.py:24
  11.9 4.0 %collective-permute-start = (bf16[1,1,256,256]{2,3,1,0:T(8,128)(2,1)}, bf16[1,1,256,256]{2,3,1,0:T(8,128)(2,1)S(1)}, u32[]{:S(2)}, u32[]{:S(2)}) collective-permute-start(bf16[1,1,256,256]{2,3,1,0:T(8,128)(2,1)} %copy.71), channel_id=1, source_target_pairs={{0,16},{16,0},{1,17},{17,1},{2,18},{18,2},{3,19},{19,3},{4,20},{20... | collective-permute-start | bytes 393224 | tf_op jit(solution)/shard_map/ppermute | solution.py:24
  13.6 0.7 copy-start.7
  15.9 0.7 copy-start.6
  39.3 17.9 %all-to-all-start.1 = ((bf16[256,8,128]{2,0,1:T(8,128)(2,1)}), bf16[256,8,128]{2,0,1:T(8,128)(2,1)}, u32[]{:S(2)}, u32[]{:S(2)}) async-start(bf16[256,8,128]{2,0,1:T(8,128)(2,1)} %get-tuple-element.485), calls=%async_computation.1 | async-start | bytes 1048576 | tf_op jit(solution)/shard_map/all_to_all | solution.py:159
  45.6 97.2 %reduce-scatter.2.cloned.1.call-start = ((), (), s32[]{:S(2)}) async-start(), calls=%async_computation.7 | async-start | bytes 589824 | tf_op jit(solution)/shard_map/reduce_scatter | solution.py:205
  57.2 22.1 %copy-start.8 = (s32[1,1,16,8]{2,3,1,0:T(8,128)S(1)}, s32[1,1,16,8]{2,3,1,0:T(8,128)}, u32[]{:S(2)}) copy-start(s32[1,1,16,8]{2,3,1,0:T(8,128)} %param.36) | copy-start | bytes 1540
  57.3 85.5 %copy-start.3 = (bf16[1,1,16,2048]{3,2,1,0:T(8,128)(2,1)S(1)}, bf16[1,1,16,2048]{3,2,1,0:T(8,128)(2,1)}, u32[]{:S(2)}) copy-start(bf16[1,1,16,2048]{3,2,1,0:T(8,128)(2,1)} %param.31) | copy-start | bytes 196612
  74.0 0.6 copy-start.9
  74.5 85.0 %copy-start.11 = (f32[1,1,16,8]{2,3,1,0:T(8,128)S(1)}, f32[1,1,16,8]{2,3,1,0:T(8,128)}, u32[]{:S(2)}) copy-start(f32[1,1,16,8]{2,3,1,0:T(8,128)} %param.37) | copy-start | bytes 1540
  78.6 115.8 %all-gather.3.cloned.1.call-start = ((), (), s32[]{:S(2)}) async-start(), calls=%async_computation.5 | async-start | bytes 1179648 | tf_op jit(solution)/shard_map/all_gather | solution.py:161
  146.1 91.7 %all-to-all-start.2 = ((bf16[16,16,2048]{2,1,0:T(8,128)(2,1)}), bf16[16,16,2048]{2,1,0:T(8,128)(2,1)}, u32[]{:S(2)}, u32[]{:S(2)}) async-start(bf16[16,16,2048]{2,1,0:T(8,128)(2,1)} %bitcast.131), calls=%async_computation.3 | async-start | bytes 2097152 | tf_op jit(solution)/shard_map/all_to_all | solution.py:236
  154.0 81.5 %all-gather.5.cloned.1.call-start = ((), (), s32[]{:S(2)}) async-start(), calls=%async_computation.6 | async-start | bytes 1179648 | tf_op jit(solution)/shard_map/all_gather | solution.py:162
  244.8 67.3 %all-to-all-start.3 = ((bf16[16,16,2048]{2,1,0:T(8,128)(2,1)}), bf16[16,16,2048]{2,1,0:T(8,128)(2,1)}, u32[]{:S(2)}, u32[]{:S(2)}) async-start(bf16[16,16,2048]{2,1,0:T(8,128)(2,1)} %bitcast.134), calls=%async_computation.4 | async-start | bytes 2097152 | tf_op jit(solution)/shard_map/all_to_all | solution.py:243
  260.0 2.1 copy-start.1
  265.6 1.3 copy-start.2
  272.3 2.1 copy-start.1
  277.8 1.3 copy-start.2
  284.6 2.1 copy-start.1
  290.1 1.3 copy-start.2
  296.8 2.1 copy-start.1
  302.4 1.3 copy-start.2
  305.7 11.5 %copy-start.4 = (bf16[16,2048]{1,0:T(8,128)(2,1)S(1)}, bf16[16,2048]{1,0:T(8,128)(2,1)}, u32[]{:S(2)}) copy-start(bf16[16,2048]{1,0:T(8,128)(2,1)} %reduce-scatter.2.cloned.1.call-done) | copy-start | bytes 196612
Sparse Core Ops, SparseCore 0:
  78.7 64.0 reduce-scatter.1
  144.9 49.4 all-gather.2
  196.5 38.9 all-gather.4
where the time goes:
time: 326 us; the launch traced here: 324 us
  waiting for transfers between devices  146 us (45%)
  matrix products  44 us (13%)
  local copies, waits for them, and re-layouts  40.7 us (12%)
  other arithmetic  32.3 us (10%)
  starting transfers between devices  24 us (7%)
  blocking collectives  16.7 us (5%)
  between operations  14.6 us (4%)
  loops' own time  5.96 us (2%)
    reduce_scatter x1, waiting for transfers between devices, body(): lax.psum_scatter(jnp.dot(dec_attn, w_out, preferred_element_type=jnp.floa...  61.8 us
    all_gather x1, waiting for transfers between devices, body(): value_piece = lax.all_gather(prompt_values, 'ctx', axis=2, tiled=True)  38.9 us
    all_gather x1, waiting for transfers between devices, body(): key_piece = lax.all_gather(prompt_keys, 'ctx', axis=2, tiled=True)  33.7 us
    all_to_all x1, blocking collectives, body(): lax.all_to_all(key_chosen, 'ctx', split_axis=1, concat_axis=0, tiled=True)  16.7 us
    unnamed x32, local copies, waits for them, and re-layouts  14.8 us
    dot_general x4, matrix products, prefill_compute(): jnp.einsum('hgqk,khd->hgqd', weights.astype(jnp.bfloat16), value_parts, p...  13.8 us
    dot_general x4, matrix products, prefill_compute(): jnp.einsum('qhgd,khd->hgqk', query_tensor, key_parts, preferred_element_t...  10.9 us
    all_to_all x1, waiting for transfers between devices, body(): lax.all_to_all(value_chosen, 'ctx', split_axis=1, concat_axis=0, tiled=True)  8.31 us
  transfers between devices with their start and end apart: 8, of which 6 were waited for; matrix products, arithmetic and copies ran while one was open for 22% of the time, Pallas kernels for 0%

commit v1 on v0

v1 whole, which is shorter than its diff:
```python
import functools
import math

import jax
import jax.numpy as jnp
from jax import lax
from jax.experimental import pallas as pl
from jax.experimental.pallas import tpu as pltpu
from jax.sharding import PartitionSpec as P

HEAD_SIZE = 128
QUERY_HEADS = 16
KEY_VALUE_HEADS = 2

NEGATIVE_LIMIT = -1e30
EPSILON = 1e-06
MESH = pl.DeviceIdType.MESH
VMEM_LIMIT = 60 * 1024 * 1024


def ring_place(index, count):
    odd = index % 2
    return (1 - odd) * (index // 2) + odd * (count - 1 - index // 2)


def ring_index(place, count):
    half = place // ((count + 1) // 2)
    return (1 - half) * 2 * place + half * (2 * (count - 1 - place) + 1)


def ring_gather_kernel(n, n_exp, split, *refs):
    n_in = 1 if split else 2
    ins, outs = refs[:n_in], refs[n_in : 2 * n_in]
    send_sem, recv_sem, peer_send, peer_recv, own_sem = refs[2 * n_in :]
    me = lax.axis_index("ctx")
    mine = lax.axis_index("exp") if n_exp > 1 else 0
    place = ring_place(me, n)
    hops = n // 2

    if split:
        width = ins[0].shape[1] // 2
        source = lambda part: ins[0].at[:, pl.ds(part * width, width)]
        slot = lambda part, index: outs[0].at[index, mine, :, pl.ds(part * width, width)]
    else:
        source = lambda part: ins[part]
        slot = lambda part, index: outs[part].at[index, mine]

    def neighbour(step):
        return ring_index((place + step + n) % n, n)

    barrier = pltpu.get_barrier_semaphore()
    for step in (-1, 1):
        pl.semaphore_signal(barrier, inc=1, device_id={"ctx": neighbour(step)}, device_id_type=MESH)
    for shift in range(1, n_exp):
        pl.semaphore_signal(
            barrier, inc=1, device_id={"exp": (mine + shift) % n_exp}, device_id_type=MESH
        )
    pl.semaphore_wait(barrier, 2 + n_exp - 1)

    started = {}
    peers = []

    def pass_on(part, message, src, index):
        for shift in range(1, n_exp):
            copy = pltpu.make_async_remote_copy(
                src_ref=src,
                dst_ref=slot(part, index),
                send_sem=peer_send.at[part, message, shift - 1],
                recv_sem=peer_recv.at[part, message, shift - 1],
                device_id={"exp": (mine + shift) % n_exp},
                device_id_type=MESH,
            )
            copy.start()
            peers.append(copy)

    flows = [(0, 1, hops), (1, -1, hops), (1, 1, n - 1 - hops), (0, -1, n - 1 - hops)]
    for hop in range(1, hops + 2):
        for part, step, most in flows:
            way = (step + 1) // 2
            index = ring_index((place - step * (hop - 1) + n * hop) % n, n)
            if hop > 1 and hop - 1 <= most:
                started[part, way, hop - 1].wait_recv()
            if hop <= most:
                copy = pltpu.make_async_remote_copy(
                    src_ref=source(part) if hop == 1 else slot(part, index),
                    dst_ref=slot(part, index),
                    send_sem=send_sem.at[part, way, hop - 1],
                    recv_sem=recv_sem.at[part, way, hop - 1],
                    device_id={"ctx": neighbour(step)},
                    device_id_type=MESH,
                )
                copy.start()
                started[part, way, hop] = copy
            if hop > 1 and hop - 1 <= most:
                pass_on(part, 1 + way * hops + hop - 2, slot(part, index), index)
        if hop == 1:
            own = []
            for part in range(2):
                copy = pltpu.make_async_copy(source(part), slot(part, me), own_sem.at[part])
                copy.start()
                own.append(copy)
                pass_on(part, 0, source(part), me)
    for copy in own:
        copy.wait()
    for copy in started.values():
        copy.wait_send()
    for copy in peers:
        copy.wait()


def ring_gather(arrays, n, n_exp, collective_id):
    split = len(arrays) == 1
    hops = n // 2
    outs = [jax.ShapeDtypeStruct((n, n_exp) + a.shape, a.dtype) for a in arrays]
    return pl.pallas_call(
        functools.partial(ring_gather_kernel, n, n_exp, split),
        out_shape=outs,
        in_specs=[pl.BlockSpec(memory_space=pltpu.VMEM)] * len(arrays),
        out_specs=[pl.BlockSpec(memory_space=pltpu.VMEM)] * len(arrays),
        scratch_shapes=[
            pltpu.SemaphoreType.DMA((2, 2, hops)),
            pltpu.SemaphoreType.DMA((2, 2, hops)),
            pltpu.SemaphoreType.DMA((2, 1 + 2 * hops, max(1, n_exp - 1))),
            pltpu.SemaphoreType.DMA((2, 1 + 2 * hops, max(1, n_exp - 1))),
            pltpu.SemaphoreType.DMA((2,)),
        ],
        compiler_params=pltpu.CompilerParams(collective_id=collective_id, has_side_effects=True),
        name="ring_gather",
    )(*arrays)


def attend_kernel(heads, causal, tile, info, *refs):
    if causal:
        q_ref, k_ref, v_ref, out_ref = refs
    else:
        q_ref, k_ref, v_ref, fk_ref, fv_ref, out_ref = refs
    rows = q_ref.shape[0]
    factor = HEAD_SIZE ** (-0.5) * math.log2(math.e)
    length, base = info[0], info[1]
    if causal:
        free = jnp.minimum(length, base) // tile
        limit = jnp.where(base < length, jnp.minimum(length, base + rows), 0)
    else:
        free = length // tile
        limit = length
    last = (limit + tile - 1) // tile
    free = jnp.minimum(free, last)
    queries = [q_ref[:, h * HEAD_SIZE : (h + 1) * HEAD_SIZE] for h in range(heads)]
    carry = []
    for h in range(heads):
        if causal:
            carry += [
                jnp.full((rows, 1), NEGATIVE_LIMIT, jnp.float32),
                jnp.zeros((rows, 1), jnp.float32),
                jnp.zeros((rows, HEAD_SIZE), jnp.float32),
            ]
        else:
            own = jnp.sum(
                queries[h].astype(jnp.float32) * fk_ref[...].astype(jnp.float32), -1, keepdims=True
            )
            carry += [
                own * factor,
                jnp.ones((rows, 1), jnp.float32),
                fv_ref[...].astype(jnp.float32),
            ]

    def step(masked, j, carry):
        start = pl.multiple_of(j * tile, tile)
        keys = k_ref[pl.ds(start, tile), :]
        values = v_ref[pl.ds(start, tile), :]
        if masked:
            column = start + lax.broadcasted_iota(jnp.int32, (rows, tile), 1)
            keep = column < length
            if causal:
                row = base + lax.broadcasted_iota(jnp.int32, (rows, tile), 0)
                keep = keep & (column <= row)
        result = []
        for h in range(heads):
            peak, total, weighted = carry[3 * h : 3 * h + 3]
            scores = lax.dot_general(
                queries[h], keys, (((1,), (1,)), ((), ())), preferred_element_type=jnp.float32
            )
            scores = scores * factor
            if masked:
                scores = jnp.where(keep, scores, NEGATIVE_LIMIT)
            new_peak = jnp.maximum(peak, jnp.max(scores, -1, keepdims=True))
            rescale = jnp.exp2(peak - new_peak)
            weights = jnp.exp2(scores - new_peak)
            if masked:
                weights = jnp.where(keep, weights, 0.0)
            total = rescale * total + jnp.sum(weights, -1, keepdims=True)
            weighted = rescale * weighted + jnp.dot(
                weights.astype(jnp.bfloat16), values, preferred_element_type=jnp.float32
            )
            result += [new_peak, total, weighted]
        return tuple(result)

    carry = lax.fori_loop(0, free, functools.partial(step, False), tuple(carry))
    carry = lax.fori_loop(free, last, functools.partial(step, True), carry)
    for h in range(heads):
        peak, total, weighted = carry[3 * h : 3 * h + 3]
        mixed = weighted / jnp.where(total > 0, total, 1.0)
        if causal:
            row = base + lax.broadcasted_iota(jnp.int32, (rows, HEAD_SIZE), 0)
            mixed = jnp.where(row < length, mixed, 0.0)
        out_ref[:, h * HEAD_SIZE : (h + 1) * HEAD_SIZE] = mixed.astype(jnp.bfloat16)


def attend(info, queries, keys, values, fresh=None):
    causal = fresh is None
    rows, width = queries.shape
    count = width // HEAD_SIZE
    group_width = QUERY_HEADS // KEY_VALUE_HEADS
    heads = math.gcd(count, 4)
    prompt_len = keys.shape[0]
    tile = math.gcd(prompt_len, 512)
    if causal:
        head_of = lambda i, info: (0, i * heads // group_width)
    else:
        head_of = lambda i, info: (0, info[2])
    in_specs = [
        pl.BlockSpec((rows, heads * HEAD_SIZE), lambda i, info: (0, i)),
        pl.BlockSpec((prompt_len, HEAD_SIZE), head_of),
        pl.BlockSpec((prompt_len, HEAD_SIZE), head_of),
    ]
    operands = [queries, keys, values]
    if not causal:
        in_specs += [pl.BlockSpec((rows, HEAD_SIZE), lambda i, info: (0, 0))] * 2
        operands += list(fresh)
    return pl.pallas_call(
        functools.partial(attend_kernel, heads, causal, tile),
        out_shape=jax.ShapeDtypeStruct((rows, width), jnp.bfloat16),
        grid_spec=pltpu.PrefetchScalarGridSpec(
            num_scalar_prefetch=1,
            grid=(count // heads,),
            in_specs=in_specs,
            out_specs=pl.BlockSpec((rows, heads * HEAD_SIZE), lambda i, info: (0, i)),
        ),
        compiler_params=pltpu.CompilerParams(dimension_semantics=("arbitrary",)),
        cost_estimate=pl.CostEstimate(
            flops=4 * rows * width * prompt_len,
            bytes_accessed=4 * rows * width + 4 * prompt_len * HEAD_SIZE,
            transcendentals=rows * count * prompt_len,
        ),
        name="prefill" if causal else "decode",
    )(info, *operands)


def body(
    prompt_query,
    prompt_keys,
    prompt_values,
    lengths,
    decode_query,
    fresh_keys,
    fresh_values,
    x_dec,
    w_out,
    norm_gain,
    w_gate_up,
    w_down,
    expert_ids,
    gate_weights,
):
    group_width = QUERY_HEADS // KEY_VALUE_HEADS
    my_group = lax.axis_index("group")
    ctx_index = lax.axis_index("ctx")
    n_ctx = lax.axis_size("ctx")
    n_exp = lax.axis_size("exp")
    length_mine = lax.dynamic_index_in_dim(lengths[:, 0], my_group, keepdims=False)
    token_rows = prompt_query.shape[2]
    prompt_len = token_rows * n_ctx
    local_heads = decode_query.shape[3] // HEAD_SIZE
    samples = decode_query.shape[2]
    kv_head = ctx_index * local_heads // group_width
    info = jnp.stack([length_mine, ctx_index * token_rows, kv_head]).astype(jnp.int32)
    partner = [(0, 1), (1, 0)]

    own_keys = lax.dynamic_slice_in_dim(fresh_keys[0, 0], kv_head * HEAD_SIZE, HEAD_SIZE, 1)
    own_values = lax.dynamic_slice_in_dim(fresh_values[0, 0], kv_head * HEAD_SIZE, HEAD_SIZE, 1)
    far_query, far_keys, far_values = lax.ppermute(
        (decode_query[0, 0], own_keys, own_values), "group", partner
    )

    keys, values = ring_gather((prompt_keys[0, 0], prompt_values[0, 0]), n_ctx, 1, 0)
    keys = keys.reshape(prompt_len, keys.shape[-1])
    values = values.reshape(prompt_len, values.shape[-1])

    far_attn = attend(info, far_query, keys, values, (far_keys, far_values))
    dec_attn = lax.ppermute(far_attn, "group", partner)
    row_count = x_dec.shape[2]
    shares = jnp.dot(dec_attn, w_out, preferred_element_type=jnp.float32).astype(jnp.bfloat16)
    shares = shares.reshape(n_ctx, row_count, shares.shape[1])
    shares = lax.all_to_all(shares, "ctx", split_axis=0, concat_axis=0, tiled=True)

    prompt_attn = attend(info, prompt_query[0, 0], keys, values)
    prompt_attention = prompt_attn.reshape(prompt_query.shape)

    projected = jnp.sum(shares.astype(jnp.float32), 0)
    residual = x_dec[0, 0].astype(jnp.float32) + projected
    normed = (
        residual
        * lax.rsqrt(jnp.mean(residual * residual, -1, keepdims=True) + EPSILON)
        * norm_gain.astype(jnp.float32)
    ).astype(jnp.bfloat16)
    model_width = normed.shape[1]
    top_count = expert_ids.shape[3]
    experts_all = w_gate_up.shape[0] * n_ctx * n_exp
    capacity = min(row_count, max(2, 2 * row_count * top_count // experts_all))
    every_row = capacity == row_count
    ids = expert_ids[0, 0]
    chosen = ids[:, :, None] == lax.iota(jnp.int32, experts_all)[None, None, :]
    if every_row:
        (arrived,) = ring_gather((normed,), n_ctx, n_exp, 1)
    else:
        one_hot = chosen.reshape(-1, experts_all).astype(jnp.int32)
        earlier = jnp.cumsum(one_hot, 0) - one_hot
        target = ids.reshape(-1) * capacity + jnp.sum(earlier * one_hot, 1)
        placing = (
            lax.iota(jnp.int32, experts_all * capacity)[:, None, None]
            == target.reshape(row_count, top_count)[None]
        ).any(-1)
        buffer = jnp.dot(
            placing.astype(jnp.bfloat16), normed, preferred_element_type=jnp.float32
        ).astype(jnp.bfloat16)
        buffer = buffer.reshape(experts_all, capacity, model_width)
        arrived = lax.all_to_all(buffer, ("ctx", "exp"), split_axis=0, concat_axis=0, tiled=True)
    flat_rows = arrived.reshape(-1, model_width)
    mixed = jnp.dot(flat_rows, w_gate_up[0], preferred_element_type=jnp.float32)
    hidden_units = mixed.shape[1] // 2
    hidden = (jax.nn.silu(mixed[:, :hidden_units]) * mixed[:, hidden_units:]).astype(jnp.bfloat16)
    produced = jnp.dot(hidden, w_down[0], preferred_element_type=jnp.float32).astype(jnp.bfloat16)
    outputs = produced.reshape(experts_all, capacity, model_width)
    returned = lax.all_to_all(outputs, ("ctx", "exp"), split_axis=0, concat_axis=0, tiled=True)
    gate_values = gate_weights[0, 0]
    if every_row:
        gates = jnp.sum(jnp.where(chosen, gate_values[:, :, None], 0.0), 1)
        moe = jnp.sum(returned.astype(jnp.float32) * gates.T[:, :, None], 0)
    else:
        picked = returned.reshape(experts_all * capacity, model_width)[target]
        moe = jnp.sum(
            picked.reshape(row_count, top_count, model_width).astype(jnp.float32)
            * gate_values[..., None],
            1,
        )
    out_dec = (residual + moe).astype(jnp.bfloat16).reshape(1, 1, row_count, model_width)
    return (prompt_attention, out_dec)


def solution(mesh):
    in_specs = (
        P("group", "exp", "ctx", None),
        P("group", "exp", "ctx", None),
        P("group", "exp", "ctx", None),
        P(None, "exp"),
        P("group", "exp", None, "ctx"),
        P("group", "exp", None, None),
        P("group", "exp", None, None),
        P("group", "exp", "ctx", None),
        P("ctx", None),
        P(),
        P(("ctx", "exp"), None, None),
        P(("ctx", "exp"), None, None),
        P("group", "exp", "ctx", None),
        P("group", "exp", "ctx", None),
    )
    out_specs = (P("group", "exp", "ctx", None), P("group", "exp", "ctx", None))
    return jax.shard_map(body, mesh=mesh, in_specs=in_specs, out_specs=out_specs, check_vma=False)
```

time: 326 us -> 128 us (0.39)
  waiting for transfers between devices: 146 us -> 14.4 us
  Pallas kernels: 0 us -> 79.7 us
  local copies, waits for them, and re-layouts: 40.7 us -> 3.62 us
  matrix products: 44 us -> 9.26 us
  other arithmetic: 32.3 us -> 5.43 us
  blocking collectives: 16.7 us -> 0 us
  between operations: 14.6 us -> 0.79 us
  starting transfers between devices: 24 us -> 14.2 us
  loops' own time: 5.96 us -> 0 us
    pallas_call x0 -> x4, Pallas kernels: none -> 79.7 us  [the longest x2 42.6 us: ring_gather(): pl.pallas_call(functools.partial(ring_gather_kernel, n, n_exp, split), ou...]
    all_gather x2 -> x0, waiting for transfers between devices: 72.5 us -> none  [the longest x1 38.9 us: body(): value_piece = lax.all_gather(prompt_values, 'ctx', axis=2, tiled=True)]
    reduce_scatter x1 -> x0, waiting for transfers between devices: 61.8 us -> none  [body(): lax.psum_scatter(jnp.dot(dec_attn, w_out, preferred_element_type=jnp.floa...]
    dot_general x15 -> x0, matrix products: 34.7 us -> none  [the longest x4 13.8 us: prefill_compute(): jnp.einsum('hgqk,khd->hgqd', weights.astype(jnp.bfloat16), value_parts, p...]
    all_to_all x1 -> x0, blocking collectives: 16.7 us -> none  [body(): lax.all_to_all(key_chosen, 'ctx', split_axis=1, concat_axis=0, tiled=True)]
    unnamed x32 -> x16, local copies, waits for them, and re-layouts: 14.8 us -> 0.66 us
    all_to_all x2 -> x1, starting transfers between devices: 14.2 us -> 5.49 us  [body(): lax.all_to_all(shares, 'ctx', split_axis=0, concat_axis=0, tiled=True)]
    reduce_or x9 -> x0, other arithmetic: 8.37 us -> none  [the longest x4 5.62 us: decode_step(): jnp.any(usable)]
  transfers between devices with their start and end apart: 8 -> 6, of which waited for: 6 -> 2; matrix products, arithmetic and copies ran while one was open for 22% -> 3% of each run, Pallas kernels for 0% -> 43%
where the time goes in v1:
time: 128 us; the launch traced here: 127 us
  Pallas kernels  79.7 us (62%)
  waiting for transfers between devices  14.4 us (11%)
  starting transfers between devices  14.2 us (11%)
  matrix products  9.26 us (7%)
  other arithmetic  5.43 us (4%)
  local copies, waits for them, and re-layouts  3.62 us (3%)
    pallas_call x2, Pallas kernels, ring_gather(): pl.pallas_call(functools.partial(ring_gather_kernel, n, n_exp, split), ou...  42.6 us
    pallas_call x2, Pallas kernels, attend(): pl.pallas_call(functools.partial(attend_kernel, heads, causal, tile), out...  37.1 us
    all_to_all x1, waiting for transfers between devices, body(): lax.all_to_all(shares, 'ctx', split_axis=0, concat_axis=0, tiled=True)  11.1 us
    all_to_all x1, starting transfers between devices, body(): lax.all_to_all(outputs, ('ctx', 'exp'), split_axis=0, concat_axis=0, tile...  5.92 us
    all_to_all x1, starting transfers between devices, body(): lax.all_to_all(shares, 'ctx', split_axis=0, concat_axis=0, tiled=True)  5.49 us
    dot_general x1, matrix products, body(): mixed = jnp.dot(flat_rows, w_gate_up[0], preferred_element_type=jnp.float32)  4.9 us
    ppermute x1, waiting for transfers between devices, body(): dec_attn = lax.ppermute(far_attn, 'group', partner)  3.32 us
    ppermute x3, starting transfers between devices, body(): lax.ppermute((decode_query[0, 0], own_keys, own_values), 'group', partner)  2.74 us
  transfers between devices with their start and end apart: 6, of which 2 were waited for; matrix products, arithmetic and copies ran while one was open for 3% of the time, Pallas kernels for 43%

profile of v1, /device:TPU:25, one launch (start us, length us, event | category | flops | bytes accessed | tf_op | source)
XLA Modules:
  0.0 127.4 jit_solution(12889739835943812592)
XLA Ops:
  0.6 0.0 copy-start
  0.6 0.0 copy-start.5
  0.7 0.0 copy-start.1
  0.7 1.3 %collective-permute-start = (bf16[128,256]{1,0:T(8,128)(2,1)}, bf16[128,256]{1,0:T(8,128)(2,1)S(1)}, u32[]{:S(2)}, u32[]{:S(2)}) collective-permute-start(bf16[128,256]{1,0:T(8,128)(2,1)} %bitcast.56), channel_id=1, source_target_pairs={{0,16},{16,0},{1,17},{17,1},{2,18},{18,2},{3,19},{19,3},{4,20},{20... | collective-permute-start | bytes 196616 | tf_op jit(solution)/shard_map/ppermute | solution.py:281
  1.9 0.8 dynamic-slice_bitcast_fusion.1
  2.7 0.3 collective-permute-start.1
  3.0 0.8 dynamic-slice_bitcast_fusion
  3.7 1.2 collective-permute-start.2
  4.9 1.2 constant_dynamic-slice_fusion
  6.2 1.2 pad_add_fusion.info
  7.3 23.3 %ring_gather.2 = (bf16[8,1,256,256]{3,2,1,0:T(8,128)(2,1)}, bf16[8,1,256,256]{3,2,1,0:T(8,128)(2,1)}) custom-call(bf16[256,256]{1,0:T(8,128)(2,1)} %bitcast.50, bf16[256,256]{1,0:T(8,128)(2,1)} %bitcast.51), custom_call_target="tpu_custom_call" | custom-call | tf_op jit(solution)/shard_map/ring_gather/pallas_call | solution.py:115
  30.7 0.0 collective-permute-done.1.refs_3_
  30.7 0.0 copy-start.3
  30.7 0.0 collective-permute-done.2.refs_4_
  30.7 0.0 copy-start.4
  30.7 0.0 collective-permute-done.refs_0_
  30.7 0.0 copy-start.2
  30.8 0.5 copy-done.3
  31.3 0.0 copy-done.4
  31.3 0.1 copy-done.2
  31.4 5.6 %decode.1 = bf16[128,256]{1,0:T(8,128)(2,1)} custom-call(s32[3]{0:T(128)} %pad_add_fusion.info, bf16[128,256]{1,0:T(8,128)(2,1)} %copy-done.2, bf16[2048,256]{1,0:T(8,128)(2,1)} %bitcast.44, bf16[2048,256]{1,0:T(8,128)(2,1)} %bitcast.46, bf16[128,128]{1,0:T(8,128)(2,1)} %copy-done.3, bf16[128,128]{1,0:T(8,128)(2,1)} %copy-done.4), custom_call_target="tpu_custom_call" | custom-call | flops 268435456 | bytes 1179648 | tf_op jit(solution)/shard_map/decode/pallas_call | solution.py:230
  37.0 0.0 collective-permute-start.3
  37.0 3.3 %collective-permute-done.3 = bf16[128,256]{1,0:T(8,128)(2,1)S(1)} collective-permute-done((bf16[128,256]{1,0:T(8,128)(2,1)}, bf16[128,256]{1,0:T(8,128)(2,1)S(1)}, u32[]{:S(2)}, u32[]{:S(2)}) %collective-permute-start.3) | collective-permute-done | bytes 65568 | tf_op jit(solution)/shard_map/ppermute | solution.py:290
  40.3 2.3 %convolution_convert_fusion = bf16[128,2048]{1,0:T(8,128)(2,1)} fusion(bf16[128,256]{1,0:T(8,128)(2,1)S(1)} %collective-permute-done.3, bf16[256,2048]{1,0:T(8,128)(2,1)} %param.22), kind=kOutput, calls=%fused_computation.5 | convolution fusion | flops 134479872 | bytes 1638400 | tf_op jit(solution)/shard_map/dot_general | solution.py:292
  42.7 5.5 %all-to-all-start = ((bf16[8,16,2048]{2,1,0:T(8,128)(2,1)}), bf16[8,16,2048]{2,1,0:T(8,128)(2,1)}, u32[]{:S(2)}, u32[]{:S(2)}) async-start(bf16[8,16,2048]{2,1,0:T(8,128)(2,1)} %bitcast.43), calls=%async_computation | async-start | bytes 1048576 | tf_op jit(solution)/shard_map/all_to_all | solution.py:294
  48.2 0.0 copy-done.5
  48.2 11.1 %all-to-all-done = bf16[8,16,2048]{2,1,0:T(8,128)(2,1)} async-done(((bf16[8,16,2048]{2,1,0:T(8,128)(2,1)}), bf16[8,16,2048]{2,1,0:T(8,128)(2,1)}, u32[]{:S(2)}, u32[]{:S(2)}) %all-to-all-start) | async-done | bytes 524320 | tf_op jit(solution)/shard_map/all_to_all | solution.py:294
  59.3 1.1 convert_reduce_fusion
  60.4 0.0 copy-done.1
  60.4 0.1 multiply_reduce_fusion.1
  60.6 0.7 multiply_convert_fusion.refs_0_
  61.3 19.3 %ring_gather.3 = bf16[8,2,16,2048]{3,2,1,0:T(8,128)(2,1)} custom-call(bf16[16,2048]{1,0:T(8,128)(2,1)} %multiply_convert_fusion.refs_0_), custom_call_target="tpu_custom_call" | custom-call | tf_op jit(solution)/shard_map/ring_gather/pallas_call | solution.py:115
  80.6 4.9 %fusion = f32[256,1536]{1,0:T(8,128)S(1)} fusion(bf16[256,2048]{1,0:T(8,128)(2,1)} %bitcast.49, bf16[1,2048,1536]{2,1,0:T(8,128)(2,1)} %param.24), kind=kOutput, calls=%fused_computation | convolution fusion | flops 1610612736 | bytes 8912896 | tf_op jit(solution)/shard_map/dot_general | solution.py:329
  85.5 0.0 copy-done
  85.5 0.0 copy-start.6
  85.5 0.0 copy-start.7
  85.5 2.0 %fusion.4 = bf16[256,2048]{1,0:T(8,128)(2,1)} fusion(bf16[1,768,2048]{2,1,0:T(8,128)(2,1)S(1)} %copy-done, f32[256,1536]{1,0:T(8,128)S(1)} %fusion), kind=kOutput, calls=%fused_computation.4 | convolution fusion | flops 807010304 | bytes 5767168 | tf_op jit(solution)/shard_map/dot_general | solution.py:332
  87.5 5.9 %all-to-all-start.1 = ((bf16[16,16,2048]{2,1,0:T(8,128)(2,1)}), bf16[16,16,2048]{2,1,0:T(8,128)(2,1)}, u32[]{:S(2)}, u32[]{:S(2)}) async-start(bf16[16,16,2048]{2,1,0:T(8,128)(2,1)} %bitcast.48), calls=%async_computation.1 | async-start | bytes 2097152 | tf_op jit(solution)/shard_map/all_to_all | solution.py:334
  93.5 0.0 copy-done.6
  93.5 0.1 copy.19
  93.5 0.0 copy-done.7
  93.5 0.1 copy.18
  93.6 0.1 select_reduce_fusion
  93.7 0.1 copy.20
  93.8 31.5 %prefill.1 = bf16[256,2048]{1,0:T(8,128)(2,1)} custom-call(s32[3]{0:T(128)} %pad_add_fusion.info, bf16[256,2048]{1,0:T(8,128)(2,1)} %bitcast.55, bf16[2048,256]{1,0:T(8,128)(2,1)} %bitcast.45, bf16[2048,256]{1,0:T(8,128)(2,1)} %bitcast.47), custom_call_target="tpu_custom_call" | custom-call | flops 4294967296 | bytes 3145728 | tf_op jit(solution)/shard_map/prefill/pallas_call | solution.py:230
  125.3 0.0 all-to-all-done.1
  125.3 1.5 %multiply_reduce_fusion = f32[16,2048]{1,0:T(8,128)S(1)} fusion(bf16[16,16,2048]{2,1,0:T(8,128)(2,1)} %all-to-all-done.1, f32[16,16]{1,0:T(8,128)S(1)} %copy.20), kind=kLoop, calls=%fused_computation.6 | loop fusion | flops 1540096 | bytes 1180672 | tf_op jit(solution)/shard_map/reduce_sum | solution.py:338
  126.8 0.6 fusion.11
  (2 shorter events, 0.0 us)
Async XLA Ops:
  0.6 84.8 %copy-start = (bf16[1,768,2048]{2,1,0:T(8,128)(2,1)S(1)}, bf16[1,768,2048]{2,1,0:T(8,128)(2,1)}, u32[]{:S(2)}) copy-start(bf16[1,768,2048]{2,1,0:T(8,128)(2,1)} %param.25) | copy-start | bytes 9437188
  0.6 47.5 %copy-start.5 = (bf16[2048]{0:T(1024)(128)(2,1)S(1)}, bf16[2048]{0:T(1024)(128)(2,1)}, u32[]{:S(2)}) copy-start(bf16[2048]{0:T(1024)(128)(2,1)} %param.23) | copy-start | bytes 12292
  0.7 59.7 %copy-start.1 = (bf16[1,1,16,2048]{3,2,1,0:T(8,128)(2,1)S(1)}, bf16[1,1,16,2048]{3,2,1,0:T(8,128)(2,1)}, u32[]{:S(2)}) copy-start(bf16[1,1,16,2048]{3,2,1,0:T(8,128)(2,1)} %param.21) | copy-start | bytes 196612
  0.7 30.1 %collective-permute-start = (bf16[128,256]{1,0:T(8,128)(2,1)}, bf16[128,256]{1,0:T(8,128)(2,1)S(1)}, u32[]{:S(2)}, u32[]{:S(2)}) collective-permute-start(bf16[128,256]{1,0:T(8,128)(2,1)} %bitcast.56), channel_id=1, source_target_pairs={{0,16},{16,0},{1,17},{17,1},{2,18},{18,2},{3,19},{19,3},{4,20},{20... | collective-permute-start | bytes 196616 | tf_op jit(solution)/shard_map/ppermute | solution.py:281
  2.7 28.0 %collective-permute-start.1 = (bf16[128,128]{1,0:T(8,128)(2,1)S(1)}, bf16[128,128]{1,0:T(8,128)(2,1)S(1)}, u32[]{:S(2)}, u32[]{:S(2)}) collective-permute-start(bf16[128,128]{1,0:T(8,128)(2,1)S(1)} %dynamic-slice_bitcast_fusion.1), channel_id=1, source_target_pairs={{0,16},{16,0},{1,17},{17,1},{2,18},{18,2},{3,19},{19,3},{4,20},{20... | collective-permute-start | bytes 98312 | tf_op jit(solution)/shard_map/ppermute | solution.py:281
  3.7 27.0 %collective-permute-start.2 = (bf16[128,128]{1,0:T(8,128)(2,1)S(1)}, bf16[128,128]{1,0:T(8,128)(2,1)S(1)}, u32[]{:S(2)}, u32[]{:S(2)}) collective-permute-start(bf16[128,128]{1,0:T(8,128)(2,1)S(1)} %dynamic-slice_bitcast_fusion), channel_id=1, source_target_pairs={{0,16},{16,0},{1,17},{17,1},{2,18},{18,2},{3,19},{19,3},{4,20},{20... | collective-permute-start | bytes 98312 | tf_op jit(solution)/shard_map/ppermute | solution.py:281
  30.7 0.6 copy-start.3
  30.7 0.6 copy-start.4
  30.7 0.6 copy-start.2
  37.0 3.3 %collective-permute-start.3 = (bf16[128,256]{1,0:T(8,128)(2,1)}, bf16[128,256]{1,0:T(8,128)(2,1)S(1)}, u32[]{:S(2)}, u32[]{:S(2)}) collective-permute-start(bf16[128,256]{1,0:T(8,128)(2,1)} %decode.1), channel_id=1, source_target_pairs={{0,16},{16,0},{1,17},{17,1},{2,18},{18,2},{3,19},{19,3},{4,20},{20... | collective-permute-start | bytes 196616 | tf_op jit(solution)/shard_map/ppermute | solution.py:290
  42.7 16.6 %all-to-all-start = ((bf16[8,16,2048]{2,1,0:T(8,128)(2,1)}), bf16[8,16,2048]{2,1,0:T(8,128)(2,1)}, u32[]{:S(2)}, u32[]{:S(2)}) async-start(bf16[8,16,2048]{2,1,0:T(8,128)(2,1)} %bitcast.43), calls=%async_computation | async-start | bytes 1048576 | tf_op jit(solution)/shard_map/all_to_all | solution.py:294
  85.5 8.0 %copy-start.6 = (f32[1,1,16,8]{2,3,1,0:T(8,128)S(1)}, f32[1,1,16,8]{2,3,1,0:T(8,128)}, u32[]{:S(2)}) copy-start(f32[1,1,16,8]{2,3,1,0:T(8,128)} %param.27) | copy-start | bytes 1540
  85.5 8.0 %copy-start.7 = (s32[1,1,16,8]{2,3,1,0:T(8,128)S(1)}, s32[1,1,16,8]{2,3,1,0:T(8,128)}, u32[]{:S(2)}) copy-start(s32[1,1,16,8]{2,3,1,0:T(8,128)} %param.26) | copy-start | bytes 1540
  87.5 37.7 %all-to-all-start.1 = ((bf16[16,16,2048]{2,1,0:T(8,128)(2,1)}), bf16[16,16,2048]{2,1,0:T(8,128)(2,1)}, u32[]{:S(2)}, u32[]{:S(2)}) async-start(bf16[16,16,2048]{2,1,0:T(8,128)(2,1)} %bitcast.48), calls=%async_computation.1 | async-start | bytes 2097152 | tf_op jit(solution)/shard_map/all_to_all | solution.py:334

commit v2 on v1

--- a/solution.py
+++ b/solution.py
@@ -129,40 +129,167 @@
     )(*arrays)
 
 
-def attend_kernel(heads, causal, tile, info, *refs):
-    if causal:
-        q_ref, k_ref, v_ref, out_ref = refs
-    else:
-        q_ref, k_ref, v_ref, fk_ref, fv_ref, out_ref = refs
+def ring_decode_kernel(n, local_heads, *refs):
+    (k_ref, v_ref, q_ref, fk_ref, fv_ref, lengths) = refs[:6]
+    k_out, v_out, attn_out = refs[6:9]
+    (far_q, far_k, far_v, near_attn, send_sem, recv_sem, swap_send, swap_recv, own_sem) = refs[9:]
+    group = lax.axis_index("group")
+    me = lax.axis_index("ctx")
+    place = ring_place(me, n)
+    hops = n // 2
+    group_width = QUERY_HEADS // KEY_VALUE_HEADS
+    column = pl.multiple_of(me * local_heads // group_width * HEAD_SIZE, HEAD_SIZE)
+    head_columns = pl.ds(column, HEAD_SIZE)
+    ins, outs = (k_ref, v_ref), (k_out, v_out)
+    rows = k_ref.shape[0]
+    samples = q_ref.shape[0]
+    factor = HEAD_SIZE ** (-0.5) * math.log2(math.e)
+
+    def neighbour(step):
+        return ring_index((place + step + n) % n, n)
+
+    barrier = pltpu.get_barrier_semaphore()
+    for step in (-1, 1):
+        pl.semaphore_signal(barrier, inc=1, device_id={"ctx": neighbour(step)}, device_id_type=MESH)
+    pl.semaphore_signal(barrier, inc=1, device_id={"group": 1 - group}, device_id_type=MESH)
+    pl.semaphore_wait(barrier, 3)
+
+    def swap(number, src, dst):
+        return pltpu.make_async_remote_copy(
+            src_ref=src,
+            dst_ref=dst,
+            send_sem=swap_send.at[number],
+            recv_sem=swap_recv.at[number],
+            device_id={"group": 1 - group},
+            device_id_type=MESH,
+        )
+
+    swaps = [
+        swap(0, q_ref, far_q),
+        swap(1, fk_ref.at[:, head_columns], far_k),
+        swap(2, fv_ref.at[:, head_columns], far_v),
+    ]
+    flows = [(0, 1, hops), (1, -1, hops), (1, 1, n - 1 - hops), (0, -1, n - 1 - hops)]
+    started = {}
+
+    def send(hop):
+        for part, step, most in flows:
+            way = (step + 1) // 2
+            if 1 < hop <= most + 1:
+                started[part, way, hop - 1].wait_recv()
+            if hop <= most:
+                index = ring_index((place - step * (hop - 1) + n * hop) % n, n)
+                copy = pltpu.make_async_remote_copy(
+                    src_ref=ins[part] if hop == 1 else outs[part].at[index],
+                    dst_ref=outs[part].at[index],
+                    send_sem=send_sem.at[part, way, hop - 1],
+                    recv_sem=recv_sem.at[part, way, hop - 1],
+                    device_id={"ctx": neighbour(step)},
+                    device_id_type=MESH,
+                )
+                copy.start()
+                started[part, way, hop] = copy
+
+    send(1)
+    for copy in swaps:
+        copy.start()
+    own = [
+        pltpu.make_async_copy(ins[part], outs[part].at[me], own_sem.at[part]) for part in range(2)
+    ]
+    for copy in own:
+        copy.start()
+    length = lengths[group, 0]
+    for copy in swaps:
+        copy.wait()
+    queries = jnp.concatenate(
+        [far_q[:, h * HEAD_SIZE : (h + 1) * HEAD_SIZE] for h in range(local_heads)], 0
+    )
+    fresh_k = jnp.concatenate([far_k[...].astype(jnp.float32)] * local_heads, 0)
+    fresh_v = jnp.concatenate([far_v[...].astype(jnp.float32)] * local_heads, 0)
+    peak = jnp.sum(queries.astype(jnp.float32) * fresh_k, -1, keepdims=True) * factor
+    state = (peak, jnp.ones_like(peak), fresh_v)
+
+    def advance(state, keys, values, index):
+        peak, total, weighted = state
+        scores = (
+            lax.dot_general(
+                queries, keys, (((1,), (1,)), ((), ())), preferred_element_type=jnp.float32
+            )
+            * factor
+        )
+        keep = index * rows + lax.broadcasted_iota(jnp.int32, scores.shape, 1) < length
+        scores = jnp.where(keep, scores, NEGATIVE_LIMIT)
+        new_peak = jnp.maximum(peak, jnp.max(scores, -1, keepdims=True))
+        rescale = jnp.exp2(peak - new_peak)
+        weights = jnp.where(keep, jnp.exp2(scores - new_peak), 0.0)
+        total = rescale * total + jnp.sum(weights, -1, keepdims=True)
+        weighted = rescale * weighted + jnp.dot(
+            weights.astype(jnp.bfloat16), values, preferred_element_type=jnp.float32
+        )
+        return new_peak, total, weighted
+
+    state = advance(state, k_ref[:, head_columns], v_ref[:, head_columns], me)
+    for hop in range(2, hops + 2):
+        send(hop)
+        steps = (1, -1) if hop - 1 <= n - 1 - hops else (1,)
+        for step in steps:
+            index = ring_index((place - step * (hop - 1) + n * hop) % n, n)
+            state = advance(
+                state, k_out[index, :, head_columns], v_out[index, :, head_columns], index
+            )
+    peak, total, weighted = state
+    mixed = (weighted / total).astype(jnp.bfloat16)
+    for h in range(local_heads):
+        near_attn[:, h * HEAD_SIZE : (h + 1) * HEAD_SIZE] = mixed[h * samples : (h + 1) * samples]
+    back = swap(3, near_attn, attn_out)
+    back.start()
+    for copy in own:
+        copy.wait()
+    for copy in started.values():
+        copy.wait_send()
+    back.wait()
+
+
+def ring_decode(keys, values, query, fresh_keys, fresh_values, lengths, n):
+    rows, samples = keys.shape[0], query.shape[0]
+    hops = n // 2
+    gathered = jax.ShapeDtypeStruct((n,) + keys.shape, keys.dtype)
+    vmem = pl.BlockSpec(memory_space=pltpu.VMEM)
+    return pl.pallas_call(
+        functools.partial(ring_decode_kernel, n, query.shape[1] // HEAD_SIZE),
+        out_shape=[gathered, gathered, jax.ShapeDtypeStruct(query.shape, jnp.bfloat16)],
+        in_specs=[vmem] * 5 + [pl.BlockSpec(memory_space=pltpu.SMEM)],
+        out_specs=[vmem] * 3,
+        scratch_shapes=[
+            pltpu.VMEM(query.shape, jnp.bfloat16),
+            pltpu.VMEM((samples, HEAD_SIZE), jnp.bfloat16),
+            pltpu.VMEM((samples, HEAD_SIZE), jnp.bfloat16),
+            pltpu.VMEM(query.shape, jnp.bfloat16),
+            pltpu.SemaphoreType.DMA((2, 2, hops)),
+            pltpu.SemaphoreType.DMA((2, 2, hops)),
+            pltpu.SemaphoreType.DMA((4,)),
+            pltpu.SemaphoreType.DMA((4,)),
+            pltpu.SemaphoreType.DMA((2,)),
+        ],
+        compiler_params=pltpu.CompilerParams(collective_id=0, has_side_effects=True),
+        name="ring_decode",
+    )(keys, values, query, fresh_keys, fresh_values, lengths)
+
+
+def prefill_kernel(heads, tile, lengths, q_ref, k_ref, v_ref, out_ref):
     rows = q_ref.shape[0]
     factor = HEAD_SIZE ** (-0.5) * math.log2(math.e)
-    length, base = info[0], info[1]
-    if causal:
-        free = jnp.minimum(length, base) // tile
-        limit = jnp.where(base < length, jnp.minimum(length, base + rows), 0)
-    else:
-        free = length // tile
-        limit = length
+    length = lengths[lax.axis_index("group"), 0]
+    base = lax.axis_index("ctx") * rows
+    limit = jnp.where(base < length, jnp.minimum(length, base + rows), 0)
     last = (limit + tile - 1) // tile
-    free = jnp.minimum(free, last)
+    free = jnp.minimum(jnp.minimum(length, base) // tile, last)
     queries = [q_ref[:, h * HEAD_SIZE : (h + 1) * HEAD_SIZE] for h in range(heads)]
-    carry = []
-    for h in range(heads):
-        if causal:
-            carry += [
-                jnp.full((rows, 1), NEGATIVE_LIMIT, jnp.float32),
-                jnp.zeros((rows, 1), jnp.float32),
-                jnp.zeros((rows, HEAD_SIZE), jnp.float32),
-            ]
-        else:
-            own = jnp.sum(
-                queries[h].astype(jnp.float32) * fk_ref[...].astype(jnp.float32), -1, keepdims=True
-            )
-            carry += [
-                own * factor,
-                jnp.ones((rows, 1), jnp.float32),
-                fv_ref[...].astype(jnp.float32),
-            ]
+    carry = [
+        jnp.full((rows, 1), NEGATIVE_LIMIT, jnp.float32),
+        jnp.zeros((rows, 1), jnp.float32),
+        jnp.zeros((rows, HEAD_SIZE), jnp.float32),
+    ] * heads
 
     def step(masked, j, carry):
         start = pl.multiple_of(j * tile, tile)
@@ -170,17 +297,17 @@
         values = v_ref[pl.ds(start, tile), :]
         if masked:
             column = start + lax.broadcasted_iota(jnp.int32, (rows, tile), 1)
-            keep = column < length
-            if causal:
-                row = base + lax.broadcasted_iota(jnp.int32, (rows, tile), 0)
-                keep = keep & (column <= row)
+            row = base + lax.broadcasted_iota(jnp.int32, (rows, tile), 0)
+            keep = (column < length) & (column <= row)
         result = []
         for h in range(heads):
             peak, total, weighted = carry[3 * h : 3 * h + 3]
-            scores = lax.dot_general(
-                queries[h], keys, (((1,), (1,)), ((), ())), preferred_element_type=jnp.float32
+            scores = (
+                lax.dot_general(
+                    queries[h], keys, (((1,), (1,)), ((), ())), preferred_element_type=jnp.float32
+                )
+                * factor
             )
-            scores = scores * factor
             if masked:
                 scores = jnp.where(keep, scores, NEGATIVE_LIMIT)
             new_peak = jnp.maximum(peak, jnp.max(scores, -1, keepdims=True))
@@ -197,53 +324,39 @@
 
     carry = lax.fori_loop(0, free, functools.partial(step, False), tuple(carry))
     carry = lax.fori_loop(free, last, functools.partial(step, True), carry)
+    row = base + lax.broadcasted_iota(jnp.int32, (rows, HEAD_SIZE), 0)
     for h in range(heads):
         peak, total, weighted = carry[3 * h : 3 * h + 3]
         mixed = weighted / jnp.where(total > 0, total, 1.0)
-        if causal:
-            row = base + lax.broadcasted_iota(jnp.int32, (rows, HEAD_SIZE), 0)
-            mixed = jnp.where(row < length, mixed, 0.0)
+        mixed = jnp.where(row < length, mixed, 0.0)
         out_ref[:, h * HEAD_SIZE : (h + 1) * HEAD_SIZE] = mixed.astype(jnp.bfloat16)
 
 
-def attend(info, queries, keys, values, fresh=None):
-    causal = fresh is None
+def prefill(lengths, queries, keys, values):
     rows, width = queries.shape
     count = width // HEAD_SIZE
     group_width = QUERY_HEADS // KEY_VALUE_HEADS
-    heads = math.gcd(count, 4)
+    heads = math.gcd(group_width, 4)
     prompt_len = keys.shape[0]
-    tile = math.gcd(prompt_len, 512)
-    if causal:
-        head_of = lambda i, info: (0, i * heads // group_width)
-    else:
-        head_of = lambda i, info: (0, info[2])
-    in_specs = [
-        pl.BlockSpec((rows, heads * HEAD_SIZE), lambda i, info: (0, i)),
-        pl.BlockSpec((prompt_len, HEAD_SIZE), head_of),
-        pl.BlockSpec((prompt_len, HEAD_SIZE), head_of),
-    ]
-    operands = [queries, keys, values]
-    if not causal:
-        in_specs += [pl.BlockSpec((rows, HEAD_SIZE), lambda i, info: (0, 0))] * 2
-        operands += list(fresh)
+    kv_spec = pl.BlockSpec((prompt_len, HEAD_SIZE), lambda i, info: (0, i * heads // group_width))
+    q_spec = pl.BlockSpec((rows, heads * HEAD_SIZE), lambda i, info: (0, i))
     return pl.pallas_call(
-        functools.partial(attend_kernel, heads, causal, tile),
+        functools.partial(prefill_kernel, heads, math.gcd(prompt_len, 512)),
         out_shape=jax.ShapeDtypeStruct((rows, width), jnp.bfloat16),
         grid_spec=pltpu.PrefetchScalarGridSpec(
             num_scalar_prefetch=1,
             grid=(count // heads,),
-            in_specs=in_specs,
-            out_specs=pl.BlockSpec((rows, heads * HEAD_SIZE), lambda i, info: (0, i)),
+            in_specs=[q_spec, kv_spec, kv_spec],
+            out_specs=q_spec,
         ),
         compiler_params=pltpu.CompilerParams(dimension_semantics=("arbitrary",)),
         cost_estimate=pl.CostEstimate(
             flops=4 * rows * width * prompt_len,
-            bytes_accessed=4 * rows * width + 4 * prompt_len * HEAD_SIZE,
+            bytes_accessed=4 * rows * width + 4 * prompt_len * keys.shape[1],
             transcendentals=rows * count * prompt_len,
         ),
-        name="prefill" if causal else "decode",
-    )(info, *operands)
+        name="prefill",
+    )(lengths, queries, keys, values)
 
 
 def body(
@@ -262,38 +375,26 @@
     expert_ids,
     gate_weights,
 ):
-    group_width = QUERY_HEADS // KEY_VALUE_HEADS
-    my_group = lax.axis_index("group")
-    ctx_index = lax.axis_index("ctx")
     n_ctx = lax.axis_size("ctx")
     n_exp = lax.axis_size("exp")
-    length_mine = lax.dynamic_index_in_dim(lengths[:, 0], my_group, keepdims=False)
-    token_rows = prompt_query.shape[2]
-    prompt_len = token_rows * n_ctx
-    local_heads = decode_query.shape[3] // HEAD_SIZE
-    samples = decode_query.shape[2]
-    kv_head = ctx_index * local_heads // group_width
-    info = jnp.stack([length_mine, ctx_index * token_rows, kv_head]).astype(jnp.int32)
-    partner = [(0, 1), (1, 0)]
-
-    own_keys = lax.dynamic_slice_in_dim(fresh_keys[0, 0], kv_head * HEAD_SIZE, HEAD_SIZE, 1)
-    own_values = lax.dynamic_slice_in_dim(fresh_values[0, 0], kv_head * HEAD_SIZE, HEAD_SIZE, 1)
-    far_query, far_keys, far_values = lax.ppermute(
-        (decode_query[0, 0], own_keys, own_values), "group", partner
+    prompt_len = prompt_query.shape[2] * n_ctx
+    keys, values, dec_attn = ring_decode(
+        prompt_keys[0, 0],
+        prompt_values[0, 0],
+        decode_query[0, 0],
+        fresh_keys[0, 0],
+        fresh_values[0, 0],
+        lengths,
+        n_ctx,
     )
-
-    keys, values = ring_gather((prompt_keys[0, 0], prompt_values[0, 0]), n_ctx, 1, 0)
     keys = keys.reshape(prompt_len, keys.shape[-1])
     values = values.reshape(prompt_len, values.shape[-1])
-
-    far_attn = attend(info, far_query, keys, values, (far_keys, far_values))
-    dec_attn = lax.ppermute(far_attn, "group", partner)
     row_count = x_dec.shape[2]
     shares = jnp.dot(dec_attn, w_out, preferred_element_type=jnp.float32).astype(jnp.bfloat16)
     shares = shares.reshape(n_ctx, row_count, shares.shape[1])
     shares = lax.all_to_all(shares, "ctx", split_axis=0, concat_axis=0, tiled=True)
 
-    prompt_attn = attend(info, prompt_query[0, 0], keys, values)
+    prompt_attn = prefill(lengths, prompt_query[0, 0], keys, values)
     prompt_attention = prompt_attn.reshape(prompt_query.shape)
 
     projected = jnp.sum(shares.astype(jnp.float32), 0)

time: 128 us -> 117 us (0.914)
  waiting for transfers between devices: 14.4 us -> 11 us
  starting transfers between devices: 14.2 us -> 11.5 us
  local copies, waits for them, and re-layouts: 3.62 us -> 1.7 us
  Pallas kernels: 79.7 us -> 78.1 us
    pallas_call x2 -> x1, Pallas kernels: 42.6 us -> 19.3 us  [ring_gather(): pl.pallas_call(functools.partial(ring_gather_kernel, n, n_exp, split), ou...]
    pallas_call x2, Pallas kernels: 37.1 us -> 58.8 us  [the longest x1 31.5 us: prefill(): pl.pallas_call(functools.partial(prefill_kernel, heads, math.gcd(prompt_l...]
    ppermute x4 -> x0, waiting for transfers between devices: 3.33 us -> none  [the longest x1 3.32 us: body(): dec_attn = lax.ppermute(far_attn, 'group', partner)]
    dynamic_slice x3 -> x0, local copies, waits for them, and re-layouts: 2.75 us -> none  [the longest x1 1.23 us: body(): lax.dynamic_index_in_dim(lengths[:, 0], my_group, keepdims=False)]
    ppermute x4 -> x0, starting transfers between devices: 2.74 us -> none  [the longest x3 2.74 us: body(): lax.ppermute((decode_query[0, 0], own_keys, own_values), 'group', partner)]
  transfers between devices with their start and end apart: 6 -> 2, of which waited for: 2 -> 1; matrix products, arithmetic and copies ran while one was open for 3% -> 0% of each run, Pallas kernels for 43% -> 27%
where the time goes in v2:
time: 117 us
  Pallas kernels  78.1 us (67%)
  starting transfers between devices  11.5 us (10%)
  waiting for transfers between devices  11 us (9%)
  matrix products  9.31 us (8%)
  other arithmetic  4.25 us (4%)
  local copies, waits for them, and re-layouts  1.7 us (1%)
    pallas_call x1, Pallas kernels, prefill(): pl.pallas_call(functools.partial(prefill_kernel, heads, math.gcd(prompt_l...  31.5 us
    pallas_call x1, Pallas kernels, ring_decode(): pl.pallas_call(functools.partial(ring_decode_kernel, n, query.shape[1] //...  27.3 us
    pallas_call x1, Pallas kernels, ring_gather(): pl.pallas_call(functools.partial(ring_gather_kernel, n, n_exp, split), ou...  19.3 us
    all_to_all x1, waiting for transfers between devices, body(): lax.all_to_all(shares, 'ctx', split_axis=0, concat_axis=0, tiled=True)  11 us
    all_to_all x1, starting transfers between devices, body(): lax.all_to_all(outputs, ('ctx', 'exp'), split_axis=0, concat_axis=0, tile...  6 us
    all_to_all x1, starting transfers between devices, body(): lax.all_to_all(shares, 'ctx', split_axis=0, concat_axis=0, tiled=True)  5.51 us
    dot_general x1, matrix products, body(): mixed = jnp.dot(flat_rows, w_gate_up[0], preferred_element_type=jnp.float32)  4.9 us
    dot_general x1, matrix products, body(): jnp.dot(dec_attn, w_out, preferred_element_type=jnp.float32)  2.37 us
  transfers between devices with their start and end apart: 2, of which 1 were waited for; matrix products, arithmetic and copies ran while one was open for 0% of the time, Pallas kernels for 27%

profile of v2, /device:TPU:25, one launch (start us, length us, event | category | flops | bytes accessed | tf_op | source)
XLA Modules:
  0.0 116.6 jit_solution(1097985983667417963)
XLA Ops:
  0.6 0.0 copy-start
  0.6 0.0 copy-start.2
  0.7 0.0 copy-start.1
  0.7 1.5 %copy.21.refs_5_.lengths = s32[2,1]{1,0:T(2,128)} copy(s32[2,1]{0,1:T(1,128)} %param.17) | data formatting | bytes 16 | tf_op args[3]
  2.1 27.3 %ring_decode.1 = (bf16[8,256,256]{2,1,0:T(8,128)(2,1)}, bf16[8,256,256]{2,1,0:T(8,128)(2,1)}, bf16[128,256]{1,0:T(8,128)(2,1)}) custom-call(bf16[256,256]{1,0:T(8,128)(2,1)} %bitcast.41, bf16[256,256]{1,0:T(8,128)(2,1)} %bitcast.42, bf16[128,256]{1,0:T(8,128)(2,1)} %bitcast.43, bf16[128,256]{1,0:T(8,128)(2,1)} %bitcast.44, bf16[128,256]{1,0:T(8,128)(2,1)} %bitcast.45, ...), custom_call_target="tpu_custom_call" | custom-call | tf_op jit(solution)/shard_map/ring_decode/pallas_call | solution.py:258
  29.5 2.4 %convolution_convert_fusion = bf16[128,2048]{1,0:T(8,128)(2,1)} fusion(bf16[128,256]{1,0:T(8,128)(2,1)} %get-tuple-element.7, bf16[256,2048]{1,0:T(8,128)(2,1)} %param.22), kind=kOutput, calls=%fused_computation.5 | convolution fusion | flops 134479872 | bytes 1638400 | tf_op jit(solution)/shard_map/dot_general | solution.py:393
  31.8 5.5 %all-to-all-start = ((bf16[8,16,2048]{2,1,0:T(8,128)(2,1)}), bf16[8,16,2048]{2,1,0:T(8,128)(2,1)}, u32[]{:S(2)}, u32[]{:S(2)}) async-start(bf16[8,16,2048]{2,1,0:T(8,128)(2,1)} %bitcast.38), calls=%async_computation | async-start | bytes 1048576 | tf_op jit(solution)/shard_map/all_to_all | solution.py:395
  37.4 0.0 copy-done.2
  37.4 11.0 %all-to-all-done = bf16[8,16,2048]{2,1,0:T(8,128)(2,1)} async-done(((bf16[8,16,2048]{2,1,0:T(8,128)(2,1)}), bf16[8,16,2048]{2,1,0:T(8,128)(2,1)}, u32[]{:S(2)}, u32[]{:S(2)}) %all-to-all-start) | async-done | bytes 524320 | tf_op jit(solution)/shard_map/all_to_all | solution.py:395
  48.4 1.1 convert_reduce_fusion
  49.5 0.0 copy-done.1
  49.5 0.1 multiply_reduce_fusion.1
  49.6 0.7 multiply_convert_fusion.refs_0_
  50.4 19.3 %ring_gather.1 = bf16[8,2,16,2048]{3,2,1,0:T(8,128)(2,1)} custom-call(bf16[16,2048]{1,0:T(8,128)(2,1)} %multiply_convert_fusion.refs_0_), custom_call_target="tpu_custom_call" | custom-call | tf_op jit(solution)/shard_map/ring_gather/pallas_call | solution.py:115
  69.7 4.9 %fusion = f32[256,1536]{1,0:T(8,128)S(1)} fusion(bf16[256,2048]{1,0:T(8,128)(2,1)} %bitcast.40, bf16[1,2048,1536]{2,1,0:T(8,128)(2,1)} %param.24), kind=kOutput, calls=%fused_computation | convolution fusion | flops 1610612736 | bytes 8912896 | tf_op jit(solution)/shard_map/dot_general | solution.py:430
  74.6 0.0 copy-done
  74.6 0.0 copy-start.3
  74.6 0.0 copy-start.4
  74.6 2.0 %fusion.4 = bf16[256,2048]{1,0:T(8,128)(2,1)} fusion(bf16[1,768,2048]{2,1,0:T(8,128)(2,1)S(1)} %copy-done, f32[256,1536]{1,0:T(8,128)S(1)} %fusion), kind=kOutput, calls=%fused_computation.4 | convolution fusion | flops 807010304 | bytes 5767168 | tf_op jit(solution)/shard_map/dot_general | solution.py:433
  76.7 6.0 %all-to-all-start.1 = ((bf16[16,16,2048]{2,1,0:T(8,128)(2,1)}), bf16[16,16,2048]{2,1,0:T(8,128)(2,1)}, u32[]{:S(2)}, u32[]{:S(2)}) async-start(bf16[16,16,2048]{2,1,0:T(8,128)(2,1)} %bitcast.39), calls=%async_computation.1 | async-start | bytes 2097152 | tf_op jit(solution)/shard_map/all_to_all | solution.py:435
  82.7 0.0 copy-done.3
  82.7 0.1 copy.23
  82.7 0.0 copy-done.4
  82.7 0.1 copy.22
  82.8 0.1 select_reduce_fusion
  82.9 0.1 copy.24
  83.0 31.5 %prefill.1 = bf16[256,2048]{1,0:T(8,128)(2,1)} custom-call(s32[2,1]{1,0:T(2,128)} %copy.21.refs_5_.lengths, bf16[256,2048]{1,0:T(8,128)(2,1)} %bitcast.49, bf16[2048,256]{1,0:T(8,128)(2,1)} %bitcast.50, bf16[2048,256]{1,0:T(8,128)(2,1)} %bitcast.51), custom_call_target="tpu_custom_call" | custom-call | flops 4294967296 | bytes 4194304 | tf_op jit(solution)/shard_map/prefill/pallas_call | solution.py:343
  114.5 0.0 all-to-all-done.1
  114.5 1.5 %multiply_reduce_fusion = f32[16,2048]{1,0:T(8,128)S(1)} fusion(bf16[16,16,2048]{2,1,0:T(8,128)(2,1)} %all-to-all-done.1, f32[16,16]{1,0:T(8,128)S(1)} %copy.24), kind=kLoop, calls=%fused_computation.6 | loop fusion | flops 1540096 | bytes 1180672 | tf_op jit(solution)/shard_map/reduce_sum | solution.py:439
  116.0 0.6 fusion.11
  (2 shorter events, 0.0 us)
Async XLA Ops:
  0.6 74.0 %copy-start = (bf16[1,768,2048]{2,1,0:T(8,128)(2,1)S(1)}, bf16[1,768,2048]{2,1,0:T(8,128)(2,1)}, u32[]{:S(2)}) copy-start(bf16[1,768,2048]{2,1,0:T(8,128)(2,1)} %param.25) | copy-start | bytes 9437188
  0.6 36.7 %copy-start.2 = (bf16[2048]{0:T(1024)(128)(2,1)S(1)}, bf16[2048]{0:T(1024)(128)(2,1)}, u32[]{:S(2)}) copy-start(bf16[2048]{0:T(1024)(128)(2,1)} %param.23) | copy-start | bytes 12292
  0.7 48.8 %copy-start.1 = (bf16[1,1,16,2048]{3,2,1,0:T(8,128)(2,1)S(1)}, bf16[1,1,16,2048]{3,2,1,0:T(8,128)(2,1)}, u32[]{:S(2)}) copy-start(bf16[1,1,16,2048]{3,2,1,0:T(8,128)(2,1)} %param.21) | copy-start | bytes 196612
  31.8 16.5 %all-to-all-start = ((bf16[8,16,2048]{2,1,0:T(8,128)(2,1)}), bf16[8,16,2048]{2,1,0:T(8,128)(2,1)}, u32[]{:S(2)}, u32[]{:S(2)}) async-start(bf16[8,16,2048]{2,1,0:T(8,128)(2,1)} %bitcast.38), calls=%async_computation | async-start | bytes 1048576 | tf_op jit(solution)/shard_map/all_to_all | solution.py:395
  74.6 8.1 %copy-start.3 = (f32[1,1,16,8]{2,3,1,0:T(8,128)S(1)}, f32[1,1,16,8]{2,3,1,0:T(8,128)}, u32[]{:S(2)}) copy-start(f32[1,1,16,8]{2,3,1,0:T(8,128)} %param.27) | copy-start | bytes 1540
  74.6 8.1 %copy-start.4 = (s32[1,1,16,8]{2,3,1,0:T(8,128)S(1)}, s32[1,1,16,8]{2,3,1,0:T(8,128)}, u32[]{:S(2)}) copy-start(s32[1,1,16,8]{2,3,1,0:T(8,128)} %param.26) | copy-start | bytes 1540
  76.7 37.8 %all-to-all-start.1 = ((bf16[16,16,2048]{2,1,0:T(8,128)(2,1)}), bf16[16,16,2048]{2,1,0:T(8,128)(2,1)}, u32[]{:S(2)}, u32[]{:S(2)}) async-start(bf16[16,16,2048]{2,1,0:T(8,128)(2,1)} %bitcast.39), calls=%async_computation.1 | async-start | bytes 2097152 | tf_op jit(solution)/shard_map/all_to_all | solution.py:435

commit v3 on v2

--- a/solution.py
+++ b/solution.py
@@ -15,7 +15,6 @@
 NEGATIVE_LIMIT = -1e30
 EPSILON = 1e-06
 MESH = pl.DeviceIdType.MESH
-VMEM_LIMIT = 60 * 1024 * 1024
 
 
 def ring_place(index, count):
@@ -28,34 +27,46 @@
     return (1 - half) * 2 * place + half * (2 * (count - 1 - place) + 1)
 
 
-def ring_gather_kernel(n, n_exp, split, *refs):
-    n_in = 1 if split else 2
-    ins, outs = refs[:n_in], refs[n_in : 2 * n_in]
-    send_sem, recv_sem, peer_send, peer_recv, own_sem = refs[2 * n_in :]
+def experts_kernel(n, n_exp, tile, *refs):
+    (x_ref, g_ref, up_hbm, down_hbm, out_ref) = refs[:5]
+    (rows_all, gates_all, up, down, hidden, produced, arrived, summed, landed) = refs[5:14]
+    (send_sem, recv_sem, peer_send, peer_recv, own_sem, w_sem) = refs[14:20]
+    (fold_send, fold_recv, home_send, home_recv) = refs[20:]
     me = lax.axis_index("ctx")
-    mine = lax.axis_index("exp") if n_exp > 1 else 0
+    mine = lax.axis_index("exp")
     place = ring_place(me, n)
     hops = n // 2
-
-    if split:
-        width = ins[0].shape[1] // 2
-        source = lambda part: ins[0].at[:, pl.ds(part * width, width)]
-        slot = lambda part, index: outs[0].at[index, mine, :, pl.ds(part * width, width)]
-    else:
-        source = lambda part: ins[part]
-        slot = lambda part, index: outs[part].at[index, mine]
+    rows, width = x_ref.shape
+    half = width // 2
+
+    loads = [
+        pltpu.make_async_copy(up_hbm, up, w_sem.at[0]),
+        pltpu.make_async_copy(down_hbm, down, w_sem.at[1]),
+    ]
+    for copy in loads:
+        copy.start()
+
+    def source(part):
+        return g_ref if part == 2 else x_ref.at[:, pl.ds(part * half, half)]
+
+    def slot(part, index):
+        if part == 2:
+            return gates_all.at[index, mine]
+        return rows_all.at[index, mine, :, pl.ds(part * half, half)]
 
     def neighbour(step):
         return ring_index((place + step + n) % n, n)
 
     barrier = pltpu.get_barrier_semaphore()
-    for step in (-1, 1):
-        pl.semaphore_signal(barrier, inc=1, device_id={"ctx": neighbour(step)}, device_id_type=MESH)
+    for shift in range(1, n):
+        pl.semaphore_signal(
+            barrier, inc=1, device_id={"ctx": (me + shift) % n}, device_id_type=MESH
+        )
     for shift in range(1, n_exp):
         pl.semaphore_signal(
             barrier, inc=1, device_id={"exp": (mine + shift) % n_exp}, device_id_type=MESH
         )
-    pl.semaphore_wait(barrier, 2 + n_exp - 1)
+    pl.semaphore_wait(barrier, n - 1 + n_exp - 1)
 
     started = {}
     peers = []
@@ -73,12 +84,14 @@
             copy.start()
             peers.append(copy)
 
-    flows = [(0, 1, hops), (1, -1, hops), (1, 1, n - 1 - hops), (0, -1, n - 1 - hops)]
+    short = n - 1 - hops
+    flows = [(0, 1, hops), (1, -1, hops), (1, 1, short), (0, -1, short), (2, 1, hops), (2, -1, short)]
+    own = []
     for hop in range(1, hops + 2):
         for part, step, most in flows:
             way = (step + 1) // 2
             index = ring_index((place - step * (hop - 1) + n * hop) % n, n)
-            if hop > 1 and hop - 1 <= most:
+            if 1 < hop <= most + 1:
                 started[part, way, hop - 1].wait_recv()
             if hop <= most:
                 copy = pltpu.make_async_remote_copy(
@@ -91,11 +104,10 @@
                 )
                 copy.start()
                 started[part, way, hop] = copy
-            if hop > 1 and hop - 1 <= most:
+            if 1 < hop <= most + 1:
                 pass_on(part, 1 + way * hops + hop - 2, slot(part, index), index)
         if hop == 1:
-            own = []
-            for part in range(2):
+            for part in range(3):
                 copy = pltpu.make_async_copy(source(part), slot(part, me), own_sem.at[part])
                 copy.start()
                 own.append(copy)
@@ -106,27 +118,126 @@
         copy.wait_send()
     for copy in peers:
         copy.wait()
-
-
-def ring_gather(arrays, n, n_exp, collective_id):
-    split = len(arrays) == 1
+    for copy in loads:
+        copy.wait()
+
+    total = n * n_exp * rows
+    units = hidden.shape[1]
+
+    def widen(t, carry):
+        at = pl.multiple_of(t * tile, tile)
+        x = rows_all[...].reshape(total, width)
+        gate = jnp.dot(x, up[:, pl.ds(at, tile)], preferred_element_type=jnp.float32)
+        linear = jnp.dot(
+            x, up[:, pl.ds(pl.multiple_of(units + at, tile), tile)],
+            preferred_element_type=jnp.float32,
+        )
+        hidden[:, pl.ds(at, tile)] = (gate / (1.0 + jnp.exp(-gate)) * linear).astype(jnp.bfloat16)
+        return carry
+
+    lax.fori_loop(0, units // tile, widen, 0)
+
+    def narrow(t, carry):
+        at = pl.multiple_of(t * tile, tile)
+        y = jnp.dot(hidden[...], down[:, pl.ds(at, tile)], preferred_element_type=jnp.float32)
+        produced[:, :, :, pl.ds(at, tile)] = y.astype(jnp.bfloat16).reshape(n, n_exp, rows, tile)
+        return carry
+
+    lax.fori_loop(0, width // tile, narrow, 0)
+
+    order = [(me + n // 2 + turn) % n for turn in range(n)]
+    folds = {}
+    for turn in range(n):
+        for shift in range(1, n_exp):
+            to = (mine + shift) % n_exp
+            copy = pltpu.make_async_remote_copy(
+                src_ref=produced.at[order[turn], to],
+                dst_ref=arrived.at[shift - 1, turn],
+                send_sem=fold_send.at[shift - 1, turn],
+                recv_sem=fold_recv.at[shift - 1, turn],
+                device_id={"exp": to},
+                device_id_type=MESH,
+            )
+            copy.start()
+            folds[turn, shift] = copy
+
+    lane = lax.broadcasted_iota(jnp.int32, (rows, gates_all.shape[3]), 1)
+    homes = []
+    for turn in range(n):
+        index = order[turn]
+        gates = gates_all[index, mine]
+
+        def gate_of(peer):
+            picked = jnp.where(lane == me * n_exp + peer, gates, 0.0)
+            return jnp.sum(picked, -1, keepdims=True)
+
+        value = gate_of(mine) * produced[index, mine].astype(jnp.float32)
+        for shift in range(1, n_exp):
+            folds[turn, shift].wait_recv()
+            giver = (mine + n_exp - shift) % n_exp
+            value = value + gate_of(giver) * arrived[shift - 1, turn].astype(jnp.float32)
+        if turn == n - n // 2:
+            out_ref[...] = value
+        else:
+            summed[turn] = value.astype(jnp.bfloat16)
+            copy = pltpu.make_async_remote_copy(
+                src_ref=summed.at[turn],
+                dst_ref=landed.at[turn],
+                send_sem=home_send.at[turn],
+                recv_sem=home_recv.at[turn],
+                device_id={"ctx": index},
+                device_id_type=MESH,
+            )
+            copy.start()
+            homes.append((turn, copy))
+    for turn, copy in homes:
+        copy.wait_recv()
+        out_ref[...] = out_ref[...] + landed[turn].astype(jnp.float32)
+    for turn, copy in homes:
+        copy.wait_send()
+    for copy in folds.values():
+        copy.wait_send()
+
+
+def experts(normed, gates, w_gate_up, w_down, n, n_exp):
+    rows, width = normed.shape
+    units = w_down.shape[0]
     hops = n // 2
-    outs = [jax.ShapeDtypeStruct((n, n_exp) + a.shape, a.dtype) for a in arrays]
+    wide = max(1, n_exp - 1)
+    vmem = pl.BlockSpec(memory_space=pltpu.VMEM)
+    hbm = pl.BlockSpec(memory_space=pl.ANY)
+    dma = pltpu.SemaphoreType.DMA
     return pl.pallas_call(
-        functools.partial(ring_gather_kernel, n, n_exp, split),
-        out_shape=outs,
-        in_specs=[pl.BlockSpec(memory_space=pltpu.VMEM)] * len(arrays),
-        out_specs=[pl.BlockSpec(memory_space=pltpu.VMEM)] * len(arrays),
+        functools.partial(experts_kernel, n, n_exp, math.gcd(math.gcd(units, width), 256)),
+        out_shape=jax.ShapeDtypeStruct((rows, width), jnp.float32),
+        in_specs=[vmem, vmem, hbm, hbm],
+        out_specs=vmem,
         scratch_shapes=[
-            pltpu.SemaphoreType.DMA((2, 2, hops)),
-            pltpu.SemaphoreType.DMA((2, 2, hops)),
-            pltpu.SemaphoreType.DMA((2, 1 + 2 * hops, max(1, n_exp - 1))),
-            pltpu.SemaphoreType.DMA((2, 1 + 2 * hops, max(1, n_exp - 1))),
-            pltpu.SemaphoreType.DMA((2,)),
+            pltpu.VMEM((n, n_exp, rows, width), jnp.bfloat16),
+            pltpu.VMEM((n, n_exp) + gates.shape, jnp.float32),
+            pltpu.VMEM(w_gate_up.shape, jnp.bfloat16),
+            pltpu.VMEM(w_down.shape, jnp.bfloat16),
+            pltpu.VMEM((n * n_exp * rows, units), jnp.bfloat16),
+            pltpu.VMEM((n, n_exp, rows, width), jnp.bfloat16),
+            pltpu.VMEM((wide, n, rows, width), jnp.bfloat16),
+            pltpu.VMEM((n, rows, width), jnp.bfloat16),
+            pltpu.VMEM((n, rows, width), jnp.bfloat16),
+            dma((3, 2, hops)),
+            dma((3, 2, hops)),
+            dma((3, 1 + 2 * hops, wide)),
+            dma((3, 1 + 2 * hops, wide)),
+            dma((3,)),
+            dma((2,)),
+            dma((wide, n)),
+            dma((wide, n)),
+            dma((n,)),
+            dma((n,)),
         ],
-        compiler_params=pltpu.CompilerParams(collective_id=collective_id, has_side_effects=True),
-        name="ring_gather",
-    )(*arrays)
+        compiler_params=pltpu.CompilerParams(
+            collective_id=1, has_side_effects=True
+        ),
+        name="experts",
+    )(normed, gates, w_gate_up, w_down)
 
 
 def ring_decode_kernel(n, local_heads, *refs):
@@ -276,8 +387,9 @@
     )(keys, values, query, fresh_keys, fresh_values, lengths)
 
 
-def prefill_kernel(heads, tile, lengths, q_ref, k_ref, v_ref, out_ref):
+def prefill_kernel(heads, tile, lengths, q_ref, k_ref, v_ref, out_ref, held):
     rows = q_ref.shape[0]
+    lanes = HEAD_SIZE
     factor = HEAD_SIZE ** (-0.5) * math.log2(math.e)
     length = lengths[lax.axis_index("group"), 0]
     base = lax.axis_index("ctx") * rows
@@ -285,48 +397,59 @@
     last = (limit + tile - 1) // tile
     free = jnp.minimum(jnp.minimum(length, base) // tile, last)
     queries = [q_ref[:, h * HEAD_SIZE : (h + 1) * HEAD_SIZE] for h in range(heads)]
-    carry = [
-        jnp.full((rows, 1), NEGATIVE_LIMIT, jnp.float32),
-        jnp.zeros((rows, 1), jnp.float32),
-        jnp.zeros((rows, HEAD_SIZE), jnp.float32),
-    ] * heads
-
-    def step(masked, j, carry):
+
+    def score(masked, j, carry):
         start = pl.multiple_of(j * tile, tile)
         keys = k_ref[pl.ds(start, tile), :]
-        values = v_ref[pl.ds(start, tile), :]
         if masked:
             column = start + lax.broadcasted_iota(jnp.int32, (rows, tile), 1)
             row = base + lax.broadcasted_iota(jnp.int32, (rows, tile), 0)
             keep = (column < length) & (column <= row)
         result = []
         for h in range(heads):
-            peak, total, weighted = carry[3 * h : 3 * h + 3]
-            scores = (
-                lax.dot_general(
-                    queries[h], keys, (((1,), (1,)), ((), ())), preferred_element_type=jnp.float32
-                )
-                * factor
+            scores = lax.dot_general(
+                queries[h], keys, (((1,), (1,)), ((), ())), preferred_element_type=jnp.float32
             )
             if masked:
                 scores = jnp.where(keep, scores, NEGATIVE_LIMIT)
-            new_peak = jnp.maximum(peak, jnp.max(scores, -1, keepdims=True))
-            rescale = jnp.exp2(peak - new_peak)
-            weights = jnp.exp2(scores - new_peak)
-            if masked:
-                weights = jnp.where(keep, weights, 0.0)
-            total = rescale * total + jnp.sum(weights, -1, keepdims=True)
-            weighted = rescale * weighted + jnp.dot(
-                weights.astype(jnp.bfloat16), values, preferred_element_type=jnp.float32
-            )
-            result += [new_peak, total, weighted]
+            held[h, :, pl.ds(start, tile)] = scores
+            peak = carry[h]
+            for at in range(0, tile, lanes):
+                peak = jnp.maximum(peak, scores[:, at : at + lanes])
+            result.append(peak)
         return tuple(result)
 
-    carry = lax.fori_loop(0, free, functools.partial(step, False), tuple(carry))
-    carry = lax.fori_loop(free, last, functools.partial(step, True), carry)
+    peaks = tuple(jnp.full((rows, lanes), NEGATIVE_LIMIT, jnp.float32) for h in range(heads))
+    peaks = lax.fori_loop(0, free, functools.partial(score, False), peaks)
+    peaks = lax.fori_loop(free, last, functools.partial(score, True), peaks)
+    peaks = [
+        jnp.broadcast_to(jnp.max(peak, -1, keepdims=True), (rows, lanes)) for peak in peaks
+    ]
+
+    def weigh(j, carry):
+        start = pl.multiple_of(j * tile, tile)
+        values = v_ref[pl.ds(start, tile), :]
+        result = []
+        for h in range(heads):
+            total, weighted = carry[2 * h : 2 * h + 2]
+            pieces = []
+            for at in range(0, tile, lanes):
+                scores = held[h, :, pl.ds(pl.multiple_of(start + at, lanes), lanes)]
+                weights = jnp.exp2((scores - peaks[h]) * factor)
+                total = total + weights
+                pieces.append(weights.astype(jnp.bfloat16))
+            weighted = weighted + jnp.dot(
+                jnp.concatenate(pieces, -1), values, preferred_element_type=jnp.float32
+            )
+            result += [total, weighted]
+        return tuple(result)
+
+    zeros = jnp.zeros((rows, HEAD_SIZE), jnp.float32)
+    carry = lax.fori_loop(0, last, weigh, (zeros,) * (2 * heads))
     row = base + lax.broadcasted_iota(jnp.int32, (rows, HEAD_SIZE), 0)
     for h in range(heads):
-        peak, total, weighted = carry[3 * h : 3 * h + 3]
+        total, weighted = carry[2 * h : 2 * h + 2]
+        total = jnp.sum(total, -1, keepdims=True)
         mixed = weighted / jnp.where(total > 0, total, 1.0)
         mixed = jnp.where(row < length, mixed, 0.0)
         out_ref[:, h * HEAD_SIZE : (h + 1) * HEAD_SIZE] = mixed.astype(jnp.bfloat16)
@@ -336,7 +459,7 @@
     rows, width = queries.shape
     count = width // HEAD_SIZE
     group_width = QUERY_HEADS // KEY_VALUE_HEADS
-    heads = math.gcd(group_width, 4)
+    heads = math.gcd(group_width, 2)
     prompt_len = keys.shape[0]
     kv_spec = pl.BlockSpec((prompt_len, HEAD_SIZE), lambda i, info: (0, i * heads // group_width))
     q_spec = pl.BlockSpec((rows, heads * HEAD_SIZE), lambda i, info: (0, i))
@@ -348,6 +471,7 @@
             grid=(count // heads,),
             in_specs=[q_spec, kv_spec, kv_spec],
             out_specs=q_spec,
+            scratch_shapes=[pltpu.VMEM((heads, rows, prompt_len), jnp.float32)],
         ),
         compiler_params=pltpu.CompilerParams(dimension_semantics=("arbitrary",)),
         cost_estimate=pl.CostEstimate(
@@ -392,9 +516,10 @@
     row_count = x_dec.shape[2]
     shares = jnp.dot(dec_attn, w_out, preferred_element_type=jnp.float32).astype(jnp.bfloat16)
     shares = shares.reshape(n_ctx, row_count, shares.shape[1])
+    keys, values, shares = lax.optimization_barrier((keys, values, shares))
     shares = lax.all_to_all(shares, "ctx", split_axis=0, concat_axis=0, tiled=True)
-
     prompt_attn = prefill(lengths, prompt_query[0, 0], keys, values)
+    shares, prompt_attn = lax.optimization_barrier((shares, prompt_attn))
     prompt_attention = prompt_attn.reshape(prompt_query.shape)
 
     projected = jnp.sum(shares.astype(jnp.float32), 0)
@@ -411,8 +536,11 @@
     every_row = capacity == row_count
     ids = expert_ids[0, 0]
     chosen = ids[:, :, None] == lax.iota(jnp.int32, experts_all)[None, None, :]
+    gate_values = gate_weights[0, 0]
     if every_row:
-        (arrived,) = ring_gather((normed,), n_ctx, n_exp, 1)
+        gates = jnp.sum(jnp.where(chosen, gate_values[:, :, None], 0.0), 1)
+        gates = jnp.pad(gates, ((0, 0), (0, -experts_all % 128)))
+        moe = experts(normed, gates, w_gate_up[0], w_down[0], n_ctx, n_exp)
     else:
         one_hot = chosen.reshape(-1, experts_all).astype(jnp.int32)
         earlier = jnp.cumsum(one_hot, 0) - one_hot
@@ -426,18 +554,15 @@
         ).astype(jnp.bfloat16)
         buffer = buffer.reshape(experts_all, capacity, model_width)
         arrived = lax.all_to_all(buffer, ("ctx", "exp"), split_axis=0, concat_axis=0, tiled=True)
-    flat_rows = arrived.reshape(-1, model_width)
-    mixed = jnp.dot(flat_rows, w_gate_up[0], preferred_element_type=jnp.float32)
-    hidden_units = mixed.shape[1] // 2
-    hidden = (jax.nn.silu(mixed[:, :hidden_units]) * mixed[:, hidden_units:]).astype(jnp.bfloat16)
-    produced = jnp.dot(hidden, w_down[0], preferred_element_type=jnp.float32).astype(jnp.bfloat16)
-    outputs = produced.reshape(experts_all, capacity, model_width)
-    returned = lax.all_to_all(outputs, ("ctx", "exp"), split_axis=0, concat_axis=0, tiled=True)
-    gate_values = gate_weights[0, 0]
-    if every_row:
-        gates = jnp.sum(jnp.where(chosen, gate_values[:, :, None], 0.0), 1)
-        moe = jnp.sum(returned.astype(jnp.float32) * gates.T[:, :, None], 0)
-    else:
+        flat_rows = arrived.reshape(-1, model_width)
+        mixed = jnp.dot(flat_rows, w_gate_up[0], preferred_element_type=jnp.float32)
+        hidden_units = mixed.shape[1] // 2
+        hidden = (jax.nn.silu(mixed[:, :hidden_units]) * mixed[:, hidden_units:]).astype(
+            jnp.bfloat16
+        )
+        produced = jnp.dot(hidden, w_down[0], preferred_element_type=jnp.float32)
+        outputs = produced.astype(jnp.bfloat16).reshape(experts_all, capacity, model_width)
+        returned = lax.all_to_all(outputs, ("ctx", "exp"), split_axis=0, concat_axis=0, tiled=True)
         picked = returned.reshape(experts_all * capacity, model_width)[target]
         moe = jnp.sum(
             picked.reshape(row_count, top_count, model_width).astype(jnp.float32)

time: 117 us -> 114 us (0.974)
  the two profiles are of different devices: /device:TPU:25 before, /device:TPU:0 now
where the time goes in v3:
time: 114 us
  Pallas kernels  100 us (88%)
  starting transfers between devices  4.45 us (4%)
  local copies, waits for them, and re-layouts  3.51 us (3%)
  other arithmetic  3.29 us (3%)
  matrix products  1.95 us (2%)
    pallas_call x1, Pallas kernels, experts(): pl.pallas_call(functools.partial(experts_kernel, n, n_exp, math.gcd(math....  56.2 us
    pallas_call x1, Pallas kernels, ring_decode(): pl.pallas_call(functools.partial(ring_decode_kernel, n, query.shape[1] //...  32 us
    pallas_call x1, Pallas kernels, prefill(): pl.pallas_call(functools.partial(prefill_kernel, heads, math.gcd(prompt_l...  12.2 us
    all_to_all x1, starting transfers between devices, body(): lax.all_to_all(shares, 'ctx', split_axis=0, concat_axis=0, tiled=True)  4.45 us
  transfers between devices with their start and end apart: 1, of which 0 were waited for; matrix products, arithmetic and copies ran while one was open for 3% of the time, Pallas kernels for 11%

profile of v3, /device:TPU:0, one launch (start us, length us, event | category | flops | bytes accessed | tf_op | source)
XLA Modules:
  0.0 114.2 jit_solution(5337080320873140790)
XLA Ops:
  0.6 0.0 copy-start
  0.6 1.4 %copy.20.refs_5_.lengths = s32[2,1]{1,0:T(2,128)} copy(s32[2,1]{0,1:T(1,128)} %param.17) | data formatting | bytes 16 | tf_op args[3]
  2.0 32.0 %ring_decode.1 = (bf16[8,256,256]{2,1,0:T(8,128)(2,1)}, bf16[8,256,256]{2,1,0:T(8,128)(2,1)}, bf16[128,256]{1,0:T(8,128)(2,1)}) custom-call(bf16[256,256]{1,0:T(8,128)(2,1)} %bitcast.29, bf16[256,256]{1,0:T(8,128)(2,1)} %bitcast.30, bf16[128,256]{1,0:T(8,128)(2,1)} %bitcast.31, bf16[128,256]{1,0:T(8,128)(2,1)} %bitcast.32, bf16[128,256]{1,0:T(8,128)(2,1)} %bitcast.33, ...), custom_call_target="tpu_custom_call" | custom-call | tf_op jit(solution)/shard_map/ring_decode/pallas_call | solution.py:369
  34.0 0.0 copy-done
  34.0 2.0 %convolution_convert_fusion = bf16[128,2048]{1,0:T(8,128)(2,1)} fusion(bf16[128,256]{1,0:T(8,128)(2,1)} %get-tuple-element.12, bf16[256,2048]{1,0:T(8,128)(2,1)S(1)} %copy-done), kind=kOutput, calls=%fused_computation | convolution fusion | flops 134479872 | bytes 1638400 | tf_op jit(solution)/shard_map/dot_general | solution.py:517
  36.0 4.4 %all-to-all-start = ((bf16[8,16,2048]{2,1,0:T(8,128)(2,1)}), bf16[8,16,2048]{2,1,0:T(8,128)(2,1)S(1)}, u32[]{:S(2)}, u32[]{:S(2)}) async-start(bf16[8,16,2048]{2,1,0:T(8,128)(2,1)} %bitcast.7), calls=%async_computation | async-start | bytes 1048576 | tf_op jit(solution)/shard_map/all_to_all | solution.py:520
  40.4 0.7 convert_element_type.27
  41.1 0.8 copy.23
  41.9 0.8 copy.22
  42.6 0.1 select_reduce_fusion
  42.7 0.6 pad.4.refs_1_
  43.3 0.0 copy-start.1
  43.3 12.2 %prefill.1 = bf16[256,2048]{1,0:T(8,128)(2,1)} custom-call(s32[2,1]{1,0:T(2,128)} %copy.20.refs_5_.lengths, bf16[256,2048]{1,0:T(8,128)(2,1)} %bitcast.36, bf16[2048,256]{1,0:T(8,128)(2,1)} %bitcast.37, bf16[2048,256]{1,0:T(8,128)(2,1)} %bitcast.38), custom_call_target="tpu_custom_call" | custom-call | flops 4294967296 | bytes 4194304 | tf_op jit(solution)/shard_map/prefill/pallas_call | solution.py:466
  55.5 0.0 all-to-all-done
  55.5 0.1 convert_reduce_fusion
  55.6 0.0 copy-done.1
  55.6 0.1 multiply_reduce_fusion
  55.7 0.7 multiply_convert_fusion.refs_0_
  56.5 56.2 %experts.1 = f32[16,2048]{1,0:T(8,128)} custom-call(bf16[16,2048]{1,0:T(8,128)(2,1)} %multiply_convert_fusion.refs_0_, f32[16,128]{1,0:T(8,128)} %pad.4.refs_1_, bf16[2048,1536]{1,0:T(8,128)(2,1)} %bitcast.27, bf16[768,2048]{1,0:T(8,128)(2,1)} %bitcast.28), custom_call_target="tpu_custom_call" | custom-call | tf_op jit(solution)/shard_map/experts/pallas_call | solution.py:210
  112.7 1.6 %fusion = bf16[1,1,16,2048]{3,2,1,0:T(8,128)(2,1)} fusion(f32[16,2048]{1,0:T(8,128)} %experts.1, f32[16,2048]{1,0:T(8,128)S(1)} %convert_reduce_fusion, bf16[1,1,16,2048]{3,2,1,0:T(8,128)(2,1)S(1)} %copy-done.1), kind=kLoop, calls=%fused_computation.6 | loop fusion | flops 131072 | bytes 393216 | tf_op jit(solution)/shard_map/reshape | solution.py:572
  (1 shorter events, 0.0 us)
Async XLA Ops:
  0.6 33.4 %copy-start = (bf16[256,2048]{1,0:T(8,128)(2,1)S(1)}, bf16[256,2048]{1,0:T(8,128)(2,1)}, u32[]{:S(2)}) copy-start(bf16[256,2048]{1,0:T(8,128)(2,1)} %param.22) | copy-start | bytes 3145732
  36.0 19.5 %all-to-all-start = ((bf16[8,16,2048]{2,1,0:T(8,128)(2,1)}), bf16[8,16,2048]{2,1,0:T(8,128)(2,1)S(1)}, u32[]{:S(2)}, u32[]{:S(2)}) async-start(bf16[8,16,2048]{2,1,0:T(8,128)(2,1)} %bitcast.7), calls=%async_computation | async-start | bytes 1048576 | tf_op jit(solution)/shard_map/all_to_all | solution.py:520
  43.3 12.3 %copy-start.1 = (bf16[1,1,16,2048]{3,2,1,0:T(8,128)(2,1)S(1)}, bf16[1,1,16,2048]{3,2,1,0:T(8,128)(2,1)}, u32[]{:S(2)}) copy-start(bf16[1,1,16,2048]{3,2,1,0:T(8,128)(2,1)} %param.21) | copy-start | bytes 196612

commit v4 on v3

--- a/solution.py
+++ b/solution.py
@@ -14,6 +14,8 @@
 
 NEGATIVE_LIMIT = -1e30
 EPSILON = 1e-06
+STACK = 4
+TILE = 1024
 MESH = pl.DeviceIdType.MESH
 
 
@@ -309,7 +311,7 @@
     ]
     for copy in own:
         copy.start()
-    length = lengths[group, 0]
+    length = lengths[group]
     for copy in swaps:
         copy.wait()
     queries = jnp.concatenate(
@@ -391,66 +393,64 @@
     rows = q_ref.shape[0]
     lanes = HEAD_SIZE
     factor = HEAD_SIZE ** (-0.5) * math.log2(math.e)
-    length = lengths[lax.axis_index("group"), 0]
+    length = lengths[lax.axis_index("group")]
     base = lax.axis_index("ctx") * rows
     limit = jnp.where(base < length, jnp.minimum(length, base + rows), 0)
     last = (limit + tile - 1) // tile
     free = jnp.minimum(jnp.minimum(length, base) // tile, last)
-    queries = [q_ref[:, h * HEAD_SIZE : (h + 1) * HEAD_SIZE] for h in range(heads)]
-
-    def score(masked, j, carry):
+    stacked = heads * rows
+    queries = jnp.concatenate(
+        [q_ref[:, h * HEAD_SIZE : (h + 1) * HEAD_SIZE] for h in range(heads)], 0
+    )
+
+    def score(masked, j, peak):
         start = pl.multiple_of(j * tile, tile)
         keys = k_ref[pl.ds(start, tile), :]
+        scores = lax.dot_general(
+            queries, keys, (((1,), (1,)), ((), ())), preferred_element_type=jnp.float32
+        )
         if masked:
             column = start + lax.broadcasted_iota(jnp.int32, (rows, tile), 1)
             row = base + lax.broadcasted_iota(jnp.int32, (rows, tile), 0)
             keep = (column < length) & (column <= row)
-        result = []
-        for h in range(heads):
-            scores = lax.dot_general(
-                queries[h], keys, (((1,), (1,)), ((), ())), preferred_element_type=jnp.float32
+            scores = jnp.concatenate(
+                [
+                    jnp.where(keep, scores[h * rows : (h + 1) * rows], NEGATIVE_LIMIT)
+                    for h in range(heads)
+                ],
+                0,
             )
-            if masked:
-                scores = jnp.where(keep, scores, NEGATIVE_LIMIT)
-            held[h, :, pl.ds(start, tile)] = scores
-            peak = carry[h]
-            for at in range(0, tile, lanes):
-                peak = jnp.maximum(peak, scores[:, at : at + lanes])
-            result.append(peak)
-        return tuple(result)
-
-    peaks = tuple(jnp.full((rows, lanes), NEGATIVE_LIMIT, jnp.float32) for h in range(heads))
-    peaks = lax.fori_loop(0, free, functools.partial(score, False), peaks)
-    peaks = lax.fori_loop(free, last, functools.partial(score, True), peaks)
-    peaks = [
-        jnp.broadcast_to(jnp.max(peak, -1, keepdims=True), (rows, lanes)) for peak in peaks
-    ]
+        held[:, pl.ds(start, tile)] = scores
+        for at in range(0, tile, lanes):
+            peak = jnp.maximum(peak, scores[:, at : at + lanes])
+        return peak
+
+    peak = jnp.full((stacked, lanes), NEGATIVE_LIMIT, jnp.float32)
+    peak = lax.fori_loop(0, free, functools.partial(score, False), peak)
+    peak = lax.fori_loop(free, last, functools.partial(score, True), peak)
+    peak = jnp.broadcast_to(jnp.max(peak, -1, keepdims=True), (stacked, lanes))
 
     def weigh(j, carry):
+        total, weighted = carry
         start = pl.multiple_of(j * tile, tile)
         values = v_ref[pl.ds(start, tile), :]
-        result = []
-        for h in range(heads):
-            total, weighted = carry[2 * h : 2 * h + 2]
-            pieces = []
-            for at in range(0, tile, lanes):
-                scores = held[h, :, pl.ds(pl.multiple_of(start + at, lanes), lanes)]
-                weights = jnp.exp2((scores - peaks[h]) * factor)
-                total = total + weights
-                pieces.append(weights.astype(jnp.bfloat16))
-            weighted = weighted + jnp.dot(
-                jnp.concatenate(pieces, -1), values, preferred_element_type=jnp.float32
-            )
-            result += [total, weighted]
-        return tuple(result)
-
-    zeros = jnp.zeros((rows, HEAD_SIZE), jnp.float32)
-    carry = lax.fori_loop(0, last, weigh, (zeros,) * (2 * heads))
+        pieces = []
+        for at in range(0, tile, lanes):
+            scores = held[:, pl.ds(pl.multiple_of(start + at, lanes), lanes)]
+            weights = jnp.exp2((scores - peak) * factor)
+            total = total + weights
+            pieces.append(weights.astype(jnp.bfloat16))
+        weighted = weighted + jnp.dot(
+            jnp.concatenate(pieces, -1), values, preferred_element_type=jnp.float32
+        )
+        return total, weighted
+
+    zeros = jnp.zeros((stacked, HEAD_SIZE), jnp.float32)
+    totals, mixes = lax.fori_loop(0, last, weigh, (zeros, zeros))
     row = base + lax.broadcasted_iota(jnp.int32, (rows, HEAD_SIZE), 0)
     for h in range(heads):
-        total, weighted = carry[2 * h : 2 * h + 2]
-        total = jnp.sum(total, -1, keepdims=True)
-        mixed = weighted / jnp.where(total > 0, total, 1.0)
+        total = jnp.sum(totals[h * rows : (h + 1) * rows], -1, keepdims=True)
+        mixed = mixes[h * rows : (h + 1) * rows] / jnp.where(total > 0, total, 1.0)
         mixed = jnp.where(row < length, mixed, 0.0)
         out_ref[:, h * HEAD_SIZE : (h + 1) * HEAD_SIZE] = mixed.astype(jnp.bfloat16)
 
@@ -459,19 +459,19 @@
     rows, width = queries.shape
     count = width // HEAD_SIZE
     group_width = QUERY_HEADS // KEY_VALUE_HEADS
-    heads = math.gcd(group_width, 2)
+    heads = math.gcd(group_width, STACK)
     prompt_len = keys.shape[0]
     kv_spec = pl.BlockSpec((prompt_len, HEAD_SIZE), lambda i, info: (0, i * heads // group_width))
     q_spec = pl.BlockSpec((rows, heads * HEAD_SIZE), lambda i, info: (0, i))
     return pl.pallas_call(
-        functools.partial(prefill_kernel, heads, math.gcd(prompt_len, 512)),
+        functools.partial(prefill_kernel, heads, math.gcd(prompt_len, TILE)),
         out_shape=jax.ShapeDtypeStruct((rows, width), jnp.bfloat16),
         grid_spec=pltpu.PrefetchScalarGridSpec(
             num_scalar_prefetch=1,
             grid=(count // heads,),
             in_specs=[q_spec, kv_spec, kv_spec],
             out_specs=q_spec,
-            scratch_shapes=[pltpu.VMEM((heads, rows, prompt_len), jnp.float32)],
+            scratch_shapes=[pltpu.VMEM((heads * rows, prompt_len), jnp.float32)],
         ),
         compiler_params=pltpu.CompilerParams(dimension_semantics=("arbitrary",)),
         cost_estimate=pl.CostEstimate(
@@ -508,7 +508,7 @@
         decode_query[0, 0],
         fresh_keys[0, 0],
         fresh_values[0, 0],
-        lengths,
+        lengths[:, 0],
         n_ctx,
     )
     keys = keys.reshape(prompt_len, keys.shape[-1])
@@ -518,7 +518,7 @@
     shares = shares.reshape(n_ctx, row_count, shares.shape[1])
     keys, values, shares = lax.optimization_barrier((keys, values, shares))
     shares = lax.all_to_all(shares, "ctx", split_axis=0, concat_axis=0, tiled=True)
-    prompt_attn = prefill(lengths, prompt_query[0, 0], keys, values)
+    prompt_attn = prefill(lengths[:, 0], prompt_query[0, 0], keys, values)
     shares, prompt_attn = lax.optimization_barrier((shares, prompt_attn))
     prompt_attention = prompt_attn.reshape(prompt_query.shape)
 

time: 114 us -> 105 us (0.921)
  Pallas kernels: 100 us -> 92.5 us
  local copies, waits for them, and re-layouts: 3.51 us -> 2.13 us
    pallas_call x1, Pallas kernels: 56.2 us -> 47 us  [experts(): pl.pallas_call(functools.partial(experts_kernel, n, n_exp, math.gcd(math....]
    unnamed x5 -> x4, local copies, waits for them, and re-layouts: 1.4 us -> 0.01 us
    pallas_call x1, Pallas kernels: 12.2 us -> 13.4 us  [prefill(): pl.pallas_call(functools.partial(prefill_kernel, heads, math.gcd(prompt_l...]
  transfers between devices with their start and end apart: 1 -> 1, of which waited for: 0 -> 0; matrix products, arithmetic and copies ran while one was open for 3% -> 3% of each run, Pallas kernels for 11% -> 13%
where the time goes in v4:
time: 105 us
  Pallas kernels  92.5 us (88%)
  starting transfers between devices  4.45 us (4%)
  other arithmetic  3.29 us (3%)
  local copies, waits for them, and re-layouts  2.13 us (2%)
  matrix products  1.95 us (2%)
    pallas_call x1, Pallas kernels, experts(): pl.pallas_call(functools.partial(experts_kernel, n, n_exp, math.gcd(math....  47 us
    pallas_call x1, Pallas kernels, ring_decode(): pl.pallas_call(functools.partial(ring_decode_kernel, n, query.shape[1] //...  32.1 us
    pallas_call x1, Pallas kernels, prefill(): pl.pallas_call(functools.partial(prefill_kernel, heads, math.gcd(prompt_l...  13.4 us
    all_to_all x1, starting transfers between devices, body(): lax.all_to_all(shares, 'ctx', split_axis=0, concat_axis=0, tiled=True)  4.45 us
  transfers between devices with their start and end apart: 1, of which 0 were waited for; matrix products, arithmetic and copies ran while one was open for 3% of the time, Pallas kernels for 13%

profile of v4, /device:TPU:0, one launch (start us, length us, event | category | flops | bytes accessed | tf_op | source)
XLA Modules:
  0.0 105.0 jit_solution(13289120097137422693)
XLA Ops:
  0.6 0.0 copy-start
  0.6 32.1 %ring_decode.1 = (bf16[8,256,256]{2,1,0:T(8,128)(2,1)}, bf16[8,256,256]{2,1,0:T(8,128)(2,1)}, bf16[128,256]{1,0:T(8,128)(2,1)}) custom-call(bf16[256,256]{1,0:T(8,128)(2,1)} %bitcast.30, bf16[256,256]{1,0:T(8,128)(2,1)} %bitcast.31, bf16[128,256]{1,0:T(8,128)(2,1)} %bitcast.32, bf16[128,256]{1,0:T(8,128)(2,1)} %bitcast.33, bf16[128,256]{1,0:T(8,128)(2,1)} %bitcast.34, ...), custom_call_target="tpu_custom_call" | custom-call | tf_op jit(solution)/shard_map/ring_decode/pallas_call | solution.py:371
  32.7 0.0 copy-done
  32.7 1.9 %convolution_convert_fusion = bf16[128,2048]{1,0:T(8,128)(2,1)} fusion(bf16[128,256]{1,0:T(8,128)(2,1)} %get-tuple-element.12, bf16[256,2048]{1,0:T(8,128)(2,1)S(1)} %copy-done), kind=kOutput, calls=%fused_computation | convolution fusion | flops 134479872 | bytes 1638400 | tf_op jit(solution)/shard_map/dot_general | solution.py:517
  34.7 4.5 %all-to-all-start = ((bf16[8,16,2048]{2,1,0:T(8,128)(2,1)}), bf16[8,16,2048]{2,1,0:T(8,128)(2,1)S(1)}, u32[]{:S(2)}, u32[]{:S(2)}) async-start(bf16[8,16,2048]{2,1,0:T(8,128)(2,1)} %bitcast.8), calls=%async_computation | async-start | bytes 1048576 | tf_op jit(solution)/shard_map/all_to_all | solution.py:520
  39.1 0.7 convert_element_type.27
  39.8 0.8 copy.19
  40.6 0.8 copy.18
  41.3 0.1 select_reduce_fusion
  41.5 0.6 pad.4.refs_1_
  42.1 0.0 copy-start.1
  42.1 13.4 %prefill.1 = bf16[256,2048]{1,0:T(8,128)(2,1)} custom-call(s32[2]{0:T(128)} %bitcast.38, bf16[256,2048]{1,0:T(8,128)(2,1)} %bitcast.39, bf16[2048,256]{1,0:T(8,128)(2,1)} %bitcast.40, bf16[2048,256]{1,0:T(8,128)(2,1)} %bitcast.41), custom_call_target="tpu_custom_call" | custom-call | flops 4294967296 | bytes 4194304 | tf_op jit(solution)/shard_map/prefill/pallas_call | solution.py:466
  55.4 0.0 all-to-all-done
  55.4 0.1 convert_reduce_fusion
  55.5 0.0 copy-done.1
  55.5 0.1 multiply_reduce_fusion
  55.7 0.7 multiply_convert_fusion.refs_0_
  56.4 47.0 %experts.1 = f32[16,2048]{1,0:T(8,128)} custom-call(bf16[16,2048]{1,0:T(8,128)(2,1)} %multiply_convert_fusion.refs_0_, f32[16,128]{1,0:T(8,128)} %pad.4.refs_1_, bf16[2048,1536]{1,0:T(8,128)(2,1)} %bitcast.28, bf16[768,2048]{1,0:T(8,128)(2,1)} %bitcast.29), custom_call_target="tpu_custom_call" | custom-call | tf_op jit(solution)/shard_map/experts/pallas_call | solution.py:212
  103.4 1.6 %fusion = bf16[1,1,16,2048]{3,2,1,0:T(8,128)(2,1)} fusion(f32[16,2048]{1,0:T(8,128)} %experts.1, f32[16,2048]{1,0:T(8,128)S(1)} %convert_reduce_fusion, bf16[1,1,16,2048]{3,2,1,0:T(8,128)(2,1)S(1)} %copy-done.1), kind=kLoop, calls=%fused_computation.6 | loop fusion | flops 131072 | bytes 393216 | tf_op jit(solution)/shard_map/reshape | solution.py:572
  (1 shorter events, 0.0 us)
Async XLA Ops:
  0.6 32.1 %copy-start = (bf16[256,2048]{1,0:T(8,128)(2,1)S(1)}, bf16[256,2048]{1,0:T(8,128)(2,1)}, u32[]{:S(2)}) copy-start(bf16[256,2048]{1,0:T(8,128)(2,1)} %param.22) | copy-start | bytes 3145732
  34.7 20.7 %all-to-all-start = ((bf16[8,16,2048]{2,1,0:T(8,128)(2,1)}), bf16[8,16,2048]{2,1,0:T(8,128)(2,1)S(1)}, u32[]{:S(2)}, u32[]{:S(2)}) async-start(bf16[8,16,2048]{2,1,0:T(8,128)(2,1)} %bitcast.8), calls=%async_computation | async-start | bytes 1048576 | tf_op jit(solution)/shard_map/all_to_all | solution.py:520
  42.1 13.5 %copy-start.1 = (bf16[1,1,16,2048]{3,2,1,0:T(8,128)(2,1)S(1)}, bf16[1,1,16,2048]{3,2,1,0:T(8,128)(2,1)}, u32[]{:S(2)}) copy-start(bf16[1,1,16,2048]{3,2,1,0:T(8,128)(2,1)} %param.21) | copy-start | bytes 196612
